TPU v7x, 512 devices: a whole 4x4x16 slice. The times are simulated.
512 devices in a mesh: layer: 8 (over y_lo, x), head: 64 (over y_hi, z, core).
Axes of the slice: x: 4, y: 4 (y_hi: 2, y_lo: 2; y = y_hi * 2 + y_lo), z: 16, core: 2. Of those that a mesh axis runs over, the one named last changes fastest.
Arguments:
- queries: bfloat16 [16, 64, 512, 128], P('layer', 'head'), may hold values from -4.5 to 4.5
- keys: bfloat16 [16, 64, 512, 128], P('layer', 'head'), may hold values from -4.5 to 4.5
- head_weight: float32 [16, 40], P('layer'), may hold values from -180 to 180
- slot_head: int32 [64], P('head'), may hold values from 0 to 40, as said below
- target: int32 [512, 512], P('head'), may hold values 0 or 1
Outputs:
- query_grad: bfloat16 [16, 64, 512, 128], P('layer', 'head')
- key_grad: bfloat16 [16, 64, 512, 128], P('layer', 'head')
- weight_grad: float32 [16, 64], P('layer', 'head')
Inputs may be any that keep to these rules, and one draw needn't show every extreme that they name: `slot_head`: each head 0 to 39 is held by exactly one slot; every other slot holds 40.
All inputs are finite; a program needn't handle non-finite values. No bound on the sum of `target` on one device may be relied on, other than what follows from the above.
Results may differ from a plain program's by a relative error of at most 0.0051.
Values sent between devices are 32-bit elements; how exact they have to be, the bound alone decides.
A program may use at most 64 MiB of HBM per device.

v0:
```python
import jax
import jax.numpy as jnp
from jax import lax
from jax.sharding import Mesh
from jax.sharding import PartitionSpec as P

HEAD = ("head_0", "head_1", "head_2")


def split_up(shard, dim, length):
    lengths = shard.shape
    tiles = shard.reshape(*lengths[:dim], length, lengths[dim] // length, *lengths[dim + 1 :])
    return jnp.moveaxis(tiles, dim, 0)


def sum_at_owner(shard, axis, dim):
    tiles = split_up(shard, dim, lax.axis_size(axis))
    arrived = lax.all_to_all(tiles, axis, split_axis=0, concat_axis=0, tiled=True)
    return arrived.sum(axis=0)


def from_everyone(shard, axis):
    copies = jnp.broadcast_to(shard, (lax.axis_size(axis), *shard.shape))
    return lax.all_to_all(copies, axis, split_axis=0, concat_axis=0, tiled=True)


def taken_together(shard, axis):
    everything = from_everyone(shard, axis)
    return jnp.sum(everything, axis=0)


def joined_along(tiles, dim):
    lengths = list(tiles.shape[1:])
    lengths[dim] *= tiles.shape[0]
    return jnp.moveaxis(tiles, 0, dim).reshape(lengths)


def stacked_from(shard, axes, sequence):
    tiles = shard
    for k in sequence:
        tiles = lax.all_gather(tiles, axes[k])
    done = sequence[::-1]
    back = [done.index(k) for k in range(len(axes))]
    tiles = tiles.transpose(*back, *range(len(axes), tiles.ndim))
    return tiles.reshape(-1, *shard.shape)


def gathered_by_axis(shard, axes, sequence, dim):
    return joined_along(stacked_from(shard, axes, sequence), dim)


def pair_maps(query, key):
    scale = query.shape[-1] ** (-0.5)
    scores = jnp.dot(query, key.T, preferred_element_type=jnp.float32) * scale
    highest = jnp.max(scores, axis=1, keepdims=True)
    expo = jnp.exp(scores - highest)
    probs = expo / jnp.sum(expo, axis=1, keepdims=True)
    sym = probs + probs.T
    rowsum = jnp.sum(sym, axis=1)
    total = jnp.sum(rowsum)
    feature = sym - rowsum[:, None] * rowsum[None, :] / total
    return (probs, rowsum, total, feature)


def pair_back(query, key, weight, error, maps):
    scale = query.shape[-1] ** (-0.5)
    probs, rowsum, total, feature = maps
    wgrad = jnp.sum(error * feature)
    gmap = weight * error
    u_vec = jnp.sum(gmap * rowsum[None, :], axis=1)
    v_vec = jnp.sum(gmap * rowsum[:, None], axis=0)
    dsym = (
        gmap - (u_vec[:, None] + v_vec[None, :]) / total + jnp.sum(rowsum * u_vec) / (total * total)
    )
    dprobs = dsym + dsym.T
    dscores = probs * (dprobs - jnp.sum(probs * dprobs, axis=1, keepdims=True))
    dscores = dscores.astype(jnp.bfloat16)
    qgrad = (jnp.dot(dscores, key, preferred_element_type=jnp.float32) * scale).astype(jnp.bfloat16)
    kgrad = lax.dot_general(
        dscores, query, (((0,), (0,)), ((), ())), preferred_element_type=jnp.float32
    )
    kgrad = (kgrad * scale).astype(jnp.bfloat16)
    return (qgrad, kgrad, wgrad)


def on_device(queries, keys, head_weight, slot_head, target):
    layer_count = queries.shape[0]
    slot_count = queries.shape[1]
    length = queries.shape[2]
    heads = head_weight.shape[1]
    onehot = (slot_head[:, None] == jnp.arange(heads, dtype=jnp.int32)[None, :]).astype(jnp.float32)
    slot_weight = jnp.dot(head_weight, onehot.T, precision=lax.Precision.HIGHEST)
    partial_value = jnp.zeros((length, length), jnp.float32)
    stored = []
    for layer_pos in range(layer_count):
        slot_pos = 0
        maps = pair_maps(queries[layer_pos, slot_pos], keys[layer_pos, slot_pos])
        partial_value = partial_value + slot_weight[layer_pos, slot_pos] * maps[3]
        stored.append(maps)
    rows = sum_at_owner(partial_value, HEAD, 0)
    rows = taken_together(rows, "layer")
    share = jax.nn.sigmoid(rows) - target.astype(jnp.float32)
    error = gathered_by_axis(share, HEAD, (0, 1, 2), 0)
    qlist = []
    klist = []
    wlist = []
    for layer_pos in range(layer_count):
        slot_pos = 0
        query = queries[layer_pos, slot_pos]
        key = keys[layer_pos, slot_pos]
        maps = stored[layer_pos * slot_count + slot_pos]
        qgrad, kgrad, wgrad = pair_back(query, key, slot_weight[layer_pos, slot_pos], error, maps)
        qrow = [qgrad]
        krow = [kgrad]
        wrow = [wgrad]
        qlist.append(jnp.stack(qrow))
        klist.append(jnp.stack(krow))
        wlist.append(jnp.stack(wrow))
    return (jnp.stack(qlist), jnp.stack(klist), jnp.stack(wlist))


def solution(mesh):
    finer = Mesh(
        mesh.devices.reshape(mesh.shape["layer"], 2, 16, 2), ("layer", "head_0", "head_1", "head_2")
    )
    placed = (
        P("layer", HEAD, None, None),
        P("layer", HEAD, None, None),
        P("layer", None),
        P(HEAD),
        P(HEAD, None),
    )
    return jax.shard_map(
        on_device,
        mesh=finer,
        in_specs=placed,
        out_specs=(P("layer", HEAD, None, None), P("layer", HEAD, None, None), P("layer", HEAD)),
        check_vma=False,
    )
```

profile of v0, /device:TPU:1, one launch (start us, length us, event | category | flops | bytes accessed | tf_op | source)
XLA Modules:
  0.0 191.2 jit_solution(1746033150466946570)
XLA Ops:
  7.2 0.0 copy-start
  7.2 0.0 copy-start.7
  7.2 0.0 copy-start.6
  7.2 0.0 all-gather.5.cloned.1.call-start
  7.2 1.4 fusion.39
  8.6 0.0 copy-done.7
  8.6 0.0 copy-done.6
  8.7 0.3 fusion.40
  9.6 0.0 copy-done
  9.6 0.1 convolution_bitcast_fusion
  9.7 0.6 fusion.38
  10.3 0.3 fusion.17
  10.7 0.3 fusion.16
  10.9 1.3 copy.37
  12.3 0.2 fusion.15
  12.5 0.2 fusion.14
  12.6 1.4 copy.35
  14.0 3.0 %fusion.36 = (f32[512]{0:T(512)S(1)}, f32[]{:T(128)}, f32[512,512]{1,0:T(8,128)S(1)}, f32[]{:T(128)}, f32[512]{0:T(512)S(1)}, /*index=5*/f32[512,512]{1,0:T(8,128)S(1)}) fusion(f32[512,512]{0,1:T(8,128)} %copy.37, f32[512,512]{1,0:T(8,128)} %copy.35, f32[512]{0:T(512)S(1)} %fusion.15, f32[512,512]{0,1:T(8,128)S(1)} %get-tuple-element.22, ...), kind=kLoop, calls=%fused_computation.71 | loop fusion | flops 2620414 | bytes 6303752 | tf_op jit(solution)/shard_map/reduce_sum | solution.py:59
  17.0 0.0 copy-start.3
  17.0 0.0 copy-start.4
  17.0 3.0 %add_bitcast_fusion = f32[64,8,512]{2,1,0:T(8,128)S(1)} fusion(f32[]{:T(128)} %bitcast.7, f32[]{:T(128)} %bitcast.5, f32[512,512]{1,0:T(8,128)S(1)} %get-tuple-element.25, f32[]{:T(128)} %get-tuple-element.23, f32[512]{0:T(512)S(1)} %get-tuple-element.24, f32[512,512]{1,0:T(8,128)S(1)} %get-tuple-element.13, f32[]{:T(128)} %get-tuple-element.10, ...), kind=kLoop, calls=%fused_computation.37 | loop fusion | flops 2359296 | bytes 3149840 | tf_op jit(solution)/shard_map/reshape | solution.py:12
  19.9 0.0 copy-done.3
  20.0 0.0 copy-done.4
  20.0 71.3 %all_to_all.10 = f32[64,8,512]{2,1,0:T(8,128)S(1)} all-to-all(f32[64,8,512]{2,1,0:T(8,128)S(1)} %add_bitcast_fusion), channel_id=1, replica_groups=mesh['layer'=8,'head_0'=2,'head_1'=16,'head_2'=2] {'head_0','head_1','he..., dimensions={0} | all-to-all | bytes 2097152 | tf_op jit(solution)/shard_map/all_to_all | solution.py:18
  91.3 0.1 reduce_sum.168
  91.4 9.5 %all_to_all.11 = f32[8,8,512]{2,1,0:T(8,128)S(1)} all-to-all(f32[8,8,512]{2,1,0:T(8,128)S(1)} %broadcast_in_dim.2), channel_id=1, replica_groups=mesh['layer'=8,'head_0'=2,'head_1'=16,'head_2'=2] {'layer'}, dimensions={0} | all-to-all | bytes 262144 | tf_op jit(solution)/shard_map/all_to_all | solution.py:24
  100.9 0.0 copy-start.11
  100.9 0.7 copy-done.11
  101.6 4.8 %all-gather = f32[16,512]{1,0:T(8,128)S(1)} all-gather(f32[8,512]{1,0:T(8,128)S(1)} %convert_subtract_fusion), channel_id=2, replica_groups=mesh['layer'=8,'head_0'=2,'head_1'=16,'head_2'=2] {'head_0'}, dimensions={0}, use_global_device_ids=true | all-gather | bytes 49152 | tf_op jit(solution)/shard_map/all_gather | solution.py:41
  106.4 29.3 %all-gather.1 = f32[32,8,512]{2,1,0:T(8,128)} all-gather(f32[2,8,512]{2,1,0:T(8,128)S(1)} %bitcast.97), channel_id=3, replica_groups=mesh['layer'=8,'head_0'=2,'head_1'=16,'head_2'=2] {'head_1'}, dimensions={0}, use_global_device_ids=true | all-gather | bytes 557056 | tf_op jit(solution)/shard_map/all_gather | solution.py:41
  135.7 0.0 all-gather.5.cloned.1.call-update
  138.2 0.1 mul.188
  138.4 0.1 mul.175
  138.5 19.2 %all-gather.5.cloned.1.call-done = f32[32,2,8,512]{3,2,1,0:T(8,128)} async-done(((f32[16,2,8,512]{3,2,1,0:T(8,128)}), f32[32,2,8,512]{3,2,1,0:T(8,128)}) %all-gather.5.cloned.1.call-update) | async-done | bytes 1048592 | tf_op jit(solution)/shard_map/all_gather | solution.py:41
  157.8 0.0 copy-start.5
  157.8 2.4 %copy.38 = f32[2,16,2,8,512]{4,3,2,1,0:T(8,128)} copy(f32[2,16,2,8,512]{4,3,0,1,2:T(8,128)} %bitcast.94) | data formatting | bytes 2097152 | tf_op jit(solution)/shard_map/transpose | solution.py:44
  160.2 0.0 copy-done.5
  160.2 1.9 multiply_reduce_fusion.4
  162.1 0.1 add.71
  162.2 0.6 multiply_reduce_fusion.6
  162.8 0.1 add.64
  162.9 0.6 multiply_reduce_fusion.7
  164.7 6.8 %fusion.12 = (f32[]{:T(128)}, f32[]{:T(128)}, f32[512,512]{1,0:T(8,128)}, f32[512,512]{1,0:T(8,128)S(1)}) fusion(f32[2,16,2,8,512]{4,3,2,1,0:T(8,128)} %copy.38, f32[512,512]{1,0:T(8,128)} %copy-done.4, f32[]{:T(128)} %get-tuple-element.23, f32[512]{0:T(512)S(1)} %get-tuple-element.24, f32[512,512]{1,0:T(8,128)} %copy-done.3, f32[]{:T(128)} %get-tuple-element.10, ...), kind=kLoop, calls=%fused_computation.25 | loop fusion | flops 5242878 | bytes 5255200 | tf_op jit(solution)/shard_map/reduce_sum | solution.py:68
  171.5 2.5 %copy.44 = f32[512,512]{0,1:T(8,128)} copy(f32[512,512]{1,0:T(8,128)} %get-tuple-element.15) | data formatting | bytes 2097152 | tf_op jit(solution)/shard_map/add | solution.py:73
  174.1 0.0 copy-start.1
  174.1 2.1 %multiply_reduce_fusion = f32[512]{0:T(512)S(1)} fusion(f32[512,512]{1,0:T(8,128)} %get-tuple-element.15, f32[512,512]{0,1:T(8,128)} %copy.44, f32[512]{0:T(512)S(1)} %fusion.17, f32[512,512]{1,0:T(8,128)S(1)} %get-tuple-element.20, f32[512]{0:T(512)S(1)} %get-tuple-element.19), kind=kLoop, calls=%fused_computation.30 | loop fusion | flops 1310208 | bytes 3151872 | tf_op jit(solution)/shard_map/reduce_sum | solution.py:76
  176.2 0.0 copy-done.1
  176.2 0.0 copy-done.2
  176.2 0.3 multiply_convert_fusion
  176.6 0.0 copy-start.8
  176.6 0.4 fusion.4
  177.0 0.6 copy-done.8
  177.6 0.9 fusion.6
  178.5 0.3 copy.41
  178.8 0.4 multiply_reduce_fusion.3
  179.2 0.4 multiply_convert_fusion.1
  179.7 0.0 copy-start.9
  179.7 0.3 fusion.5
  180.0 0.6 copy-done.9
  180.6 0.3 fusion.7
  181.0 1.9 pad_maximum_fusion.2
  182.8 0.0 copy-done.10
  182.9 0.7 pad_maximum_fusion
  183.6 0.7 pad_maximum_fusion.1
  (9 shorter events, 0.2 us)
Async XLA Ops:
  7.2 2.5 %copy-start = (f32[2,40]{1,0:T(2,128)S(1)}, f32[2,40]{1,0:T(2,128)}, u32[]{:S(2)}) copy-start(f32[2,40]{1,0:T(2,128)} %param.7) | copy-start | bytes 964
  7.2 1.5 copy-start.7
  7.2 1.5 copy-start.6
  7.2 150.6 %all-gather.5.cloned.1.call-start = ((), (), s32[]{:S(2)}) async-start(), calls=%async_computation.2 | async-start | bytes 1572864 | tf_op jit(solution)/shard_map/all_gather | solution.py:41
  17.0 3.0 %copy-start.3 = (f32[512,512]{1,0:T(8,128)}, f32[512,512]{1,0:T(8,128)S(1)}, u32[]{:S(2)}) copy-start(f32[512,512]{1,0:T(8,128)S(1)} %get-tuple-element.13) | copy-start | bytes 3145732
  17.0 3.0 %copy-start.4 = (f32[512,512]{1,0:T(8,128)}, f32[512,512]{1,0:T(8,128)S(1)}, u32[]{:S(2)}) copy-start(f32[512,512]{1,0:T(8,128)S(1)} %get-tuple-element.25) | copy-start | bytes 3145732
  100.9 0.7 copy-start.11
  157.8 2.4 %copy-start.5 = (f32[32,2,8,512]{3,2,1,0:T(8,128)S(1)}, f32[32,2,8,512]{3,2,1,0:T(8,128)}, u32[]{:S(2)}) copy-start(f32[32,2,8,512]{3,2,1,0:T(8,128)} %all-gather.5.cloned.1.call-done) | copy-start | bytes 3145732
  174.1 2.1 %copy-start.1 = (f32[512,512]{1,0:T(8,128)S(1)}, f32[512,512]{1,0:T(8,128)}, u32[]{:S(2)}) copy-start(f32[512,512]{1,0:T(8,128)} %get-tuple-element.15) | copy-start | bytes 3145732
  174.1 2.2 %copy-start.2 = (f32[512,512]{0,1:T(8,128)S(1)}, f32[512,512]{0,1:T(8,128)}, u32[]{:S(2)}) copy-start(f32[512,512]{0,1:T(8,128)} %copy.44) | copy-start | bytes 3145732
  176.6 1.0 copy-start.8
  179.7 1.0 copy-start.9
  180.6 2.2 %copy-start.10 = (bf16[1,1,512,128]{3,2,1,0:T(8,128)(2,1)S(1)}, bf16[1,1,512,128]{3,2,1,0:T(8,128)(2,1)}, u32[]{:S(2)}) copy-start(bf16[1,1,512,128]{3,2,1,0:T(8,128)(2,1)} %fusion.6) | copy-start | bytes 393220
Sparse Core Ops, SparseCore 0:
  135.8 21.8 all-gather.4
where the time goes:
time: 192 us; the launch traced here: 191 us
  blocking collectives  115 us (60%)
  other arithmetic  23.5 us (12%)
  waiting for transfers between devices  19.2 us (10%)
  between operations  18.6 us (10%)
  local copies, waits for them, and re-layouts  11.1 us (6%)
  matrix products  3.76 us (2%)
    all_to_all x1, blocking collectives, sum_at_owner(): lax.all_to_all(tiles, axis, split_axis=0, concat_axis=0, tiled=True)  71.3 us
    all_gather x2, blocking collectives, stacked_from(): tiles = lax.all_gather(tiles, axes[k])  34.1 us
    all_gather x1, waiting for transfers between devices, stacked_from(): tiles = lax.all_gather(tiles, axes[k])  19.2 us
    all_to_all x1, blocking collectives, from_everyone(): return lax.all_to_all(copies, axis, split_axis=0, concat_axis=0, tiled=True)  9.46 us
    reduce_sum x1, other arithmetic, pair_back(): wgrad = jnp.sum(error * feature)  6.83 us
  transfers between devices with their start and end apart: 1, of which 1 were waited for; matrix products, arithmetic and copies ran while one was open for 0% of the time, Pallas kernels for 0%

commit v1 on v0

v1 whole, which is shorter than its diff:
```python
import jax
import jax.numpy as jnp
from jax import lax
from jax.experimental import pallas as pl
from jax.experimental.pallas import tpu as pltpu
from jax.sharding import PartitionSpec as P

MESH = pl.DeviceIdType.MESH
F32 = jnp.float32
BF16 = jnp.bfloat16
L = 512
DH = 128
TILE = 128
TOTAL = 2.0 * L
OFF = {1: (0, 1), 2: (0, 2), 3: (1, 3), 4: (3, 0), 5: (2, 1), 6: (3, 2)}
DIAG = {0: (0, 1), 7: (3, 2)}
KEEP = (0, 0, 0, 1, 1, 0, 1, 1)
MIRROR = (1, 0, 5, 4, 2, 3, 7, 6)
MIRRORED = (1, 0, 4, 5, 3, 2, 7, 6)
MAIN = 32
ROWS = 40
OFFSETS = sorted(
    ((dx, dy) for dx in range(4) for dy in range(4) if dx or dy),
    key=lambda o: -(min(o[0], 4 - o[0]) + min(o[1], 4 - o[1])),
)


def pick(index, table):
    value = jnp.int32(table[0])
    for k in range(1, len(table)):
        value = jnp.where(index == k, jnp.int32(table[k]), value)
    return value


def slot_weights(slot_ref, hw_ref):
    hw = hw_ref[...]
    lane = lax.broadcasted_iota(jnp.int32, hw.shape, 1)
    return jnp.sum(jnp.where(lane == slot_ref[0], hw, 0.0), axis=1, keepdims=True)


def forward(w, q_ref, k_ref, p_ref, rb_ref, rr_ref, x_ref):
    scale = DH ** (-0.5)
    chunk = 64
    sums = []
    for layer in range(2):

        def body(i, csum, layer=layer):
            rows = pl.ds(pl.multiple_of(i * chunk, chunk), chunk)
            scores = lax.dot_general(
                q_ref[layer, rows, :], k_ref[layer], (((1,), (1,)), ((), ())), preferred_element_type=F32
            )
            highest = jnp.max(scores, axis=1, keepdims=True)
            expo = jnp.exp((scores - highest) * scale)
            probs = expo * (1.0 / jnp.sum(expo, axis=1, keepdims=True))
            p_ref[layer, rows, :] = probs
            return csum + jnp.sum(probs, axis=0, keepdims=True)

        csum = lax.fori_loop(0, L // chunk, body, jnp.zeros((1, L), F32))
        rowsum = 1.0 + csum
        rr_ref[layer : layer + 1, :] = rowsum
        for t in range(4):
            wide = jnp.broadcast_to(rowsum[:, t * TILE : (t + 1) * TILE], (TILE, TILE))
            rb_ref[layer, t * TILE : (t + 1) * TILE, :] = wide.T
        sums.append(rowsum * (w[layer : layer + 1, :] / TOTAL))

    def cut(t):
        return slice(t * TILE, (t + 1) * TILE)

    def half(a, b):
        return w[0:1, :] * p_ref[0, cut(a), cut(b)] + w[1:2, :] * p_ref[1, cut(a), cut(b)]

    def block(a, b):
        outer = rb_ref[0, cut(a), :] * sums[0][:, cut(b)] + rb_ref[1, cut(a), :] * sums[1][:, cut(b)]
        return half(a, b) + half(b, a).T - outer

    row = lax.broadcasted_iota(jnp.int32, (TILE, TILE), 0)
    col = lax.broadcasted_iota(jnp.int32, (TILE, TILE), 1)
    for g in range(8):
        if g in OFF:
            full = block(*OFF[g])
            extra = jnp.zeros((8, TILE), F32)
        else:
            upper = block(DIAG[g][0], DIAG[g][0])
            full = jnp.where(row < col, upper, block(DIAG[g][1], DIAG[g][1]))
            extra = jnp.sum(jnp.where(row == col, upper, 0.0), axis=0, keepdims=True)
            extra = jnp.broadcast_to(extra, (8, TILE))
        for part in range(4):
            x_ref[part % 2, 2 * g + part // 2, 0:MAIN, :] = full[part * MAIN : (part + 1) * MAIN, :]
            x_ref[part % 2, 2 * g + part // 2, MAIN:ROWS, :] = extra


def unpack(o_ref, s_ref):
    row = lax.broadcasted_iota(jnp.int32, (TILE, TILE), 0)
    col = lax.broadcasted_iota(jnp.int32, (TILE, TILE), 1)

    def cut(t):
        return slice(t * TILE, (t + 1) * TILE)

    for g in range(8):
        full = jnp.concatenate([o_ref[part % 2, 2 * g + part // 2, 0:MAIN, :] for part in range(4)], axis=0)
        if g in OFF:
            a, b = OFF[g]
            s_ref[cut(a), cut(b)] = full
            s_ref[cut(b), cut(a)] = full.T
        else:
            a, b = DIAG[g]
            turned = full.T
            diagonal = o_ref[0, 2 * g, MAIN : MAIN + 1, :]
            upper = jnp.where(row < col, full, jnp.where(row == col, diagonal, turned))
            s_ref[cut(a), cut(a)] = upper
            s_ref[cut(b), cut(b)] = jnp.where(row < col, turned, full)


def exchange_kernel(
    slot_ref, hw_ref, target_ref, q_ref, k_ref,
    p_ref, s_ref, rb_ref, rr_ref,
    x_ref, a_ref, y_ref, b_ref, z_ref, za_ref, zb_ref, t_ref, to_ref, ta_ref, tb_ref, tt_ref, piece_ref, o_ref,
    s0, r0, s1, r1, sz, rz, st, rt, s3, r3, s4, r4,
):
    layer_pos = lax.axis_index("layer")
    head_pos = lax.axis_index("head")
    x = layer_pos % 4
    y_lo = layer_pos // 4
    core = head_pos % 2
    z = (head_pos // 2) % 16
    y_hi = head_pos // 32
    y = y_hi * 2 + y_lo
    group = y_hi * 4 + x
    other = 1 - core
    mine = group * 2 + y_lo

    def device(dx=0, dy=0, dz=0, flip=False):
        nx = (x + dx) % 4
        ny = (y + dy) % 4
        nz = (z + dz) % 16
        nc = other if flip else core
        return {"layer": (ny % 2) * 4 + nx, "head": (ny // 2) * 32 + nz * 2 + nc}

    def place(dx, dy):
        nx = (x + dx) % 4
        ny = (y + dy) % 4
        return ((ny // 2) * 4 + nx) * 2 + ny % 2

    def in_group(g, c):
        return {"layer": y_lo * 4 + g % 4, "head": (g // 4) * 32 + z * 2 + c}

    partner = device(flip=True)
    sent_to = pick(group, MIRROR)
    got_from = pick(group, MIRRORED)

    barrier = pltpu.get_barrier_semaphore()
    greeted = [device(dx, dy) for dx, dy in OFFSETS]
    greeted += [device(dz=d) for d in (8, 4, -4, 2, -2, 1, -1)]
    greeted += [partner, in_group(sent_to, other), in_group(got_from, other)]
    for d in greeted:
        pl.semaphore_signal(barrier, inc=1, device_id=d, device_id_type=MESH)

    w = slot_weights(slot_ref, hw_ref)
    forward(w, q_ref, k_ref, p_ref, rb_ref, rr_ref, x_ref)

    pl.semaphore_wait(barrier, len(greeted))

    def copy(src, dst, ssem, rsem, dev):
        return pltpu.make_async_remote_copy(
            src_ref=src, dst_ref=dst, send_sem=ssem, recv_sem=rsem, device_id=dev, device_id_type=MESH
        )

    tile = target_ref.at[:, pl.ds(pl.multiple_of(x * TILE, TILE), TILE)]
    near = [(1, 4), (-1, 6), (-2, 7)]
    far = [(4, 0), (-4, 8), (8, 12)]
    t_near = [copy(tile, t_ref.at[slot], st.at[i], rt.at[i], device(dz=d)) for i, (d, slot) in enumerate(near)]
    for c in t_near:
        c.start()
    t_ref[5] = target_ref[:, pl.ds(pl.multiple_of(x * TILE, TILE), TILE)]

    swaps = []
    for i, (dx, dy) in enumerate(OFFSETS + [(0, 0)]):
        p = place(dx, dy)
        swaps.append(copy(x_ref.at[other, p], a_ref.at[p], s0.at[i], r0.at[i], partner))
        swaps[-1].start()

    plane = []
    for i, (dx, dy) in enumerate(OFFSETS):
        p = place(dx, dy)
        swaps[i].wait_recv()
        y_ref[i] = x_ref[core, p] + a_ref[p]
        plane.append(copy(y_ref.at[i], b_ref.at[i], s1.at[i], r1.at[i], device(dx, dy)))
        plane[-1].start()
    swaps[15].wait_recv()
    total = x_ref[core, mine] + a_ref[mine]

    for c in t_near:
        c.wait_recv()
    t_far = [
        copy(t_ref.at[pl.ds(4, 4)], t_ref.at[pl.ds(slot, 4)], st.at[3 + i], rt.at[3 + i], device(dz=d))
        for i, (d, slot) in enumerate(far)
    ]
    for c in t_far:
        c.start()

    for i in reversed(range(15)):
        plane[i].wait_recv()
        total = total + b_ref[i]
    z_ref[0] = total
    z_near = [
        copy(z_ref.at[0], za_ref.at[i], sz.at[i], rz.at[i], device(dz=d)) for i, d in enumerate((1, -1, -2))
    ]
    for c in z_near:
        c.start()
    for i, c in enumerate(z_near):
        c.wait_recv()
        total = total + za_ref[i]
    z_ref[1] = total
    z_far = [
        copy(z_ref.at[1], zb_ref.at[i], sz.at[3 + i], rz.at[3 + i], device(dz=d)) for i, d in enumerate((4, -4, 8))
    ]
    for c in z_far:
        c.start()

    for c in t_far:
        c.wait_recv()
    for slot in range(16):
        to_ref[(z + slot + 11) % 16] = t_ref[slot]
    keep = pick(group, KEEP)
    kept = to_ref.at[pl.ds(keep * 8, 8)]
    given = to_ref.at[pl.ds((1 - keep) * 8, 8)]
    t_plane = [
        copy(kept, ta_ref.at[core], st.at[6], rt.at[6], partner),
        copy(given, tb_ref.at[core], st.at[7], rt.at[7], in_group(sent_to, core)),
        copy(given, tb_ref.at[core], st.at[8], rt.at[8], in_group(sent_to, other)),
    ]
    for c in t_plane:
        c.start()
    ta_ref[core] = to_ref[pl.ds(keep * 8, 8)]
    copy(kept, ta_ref.at[other], st.at[6], rt.at[6], partner).wait_recv()
    copy(given, tb_ref.at[core], st.at[7], rt.at[7], in_group(sent_to, core)).wait_recv()
    copy(given, tb_ref.at[other], st.at[8], rt.at[8], in_group(sent_to, other)).wait_recv()

    def joined(ref):
        return jnp.concatenate([ref[t % 2, t // 2] for t in range(16)], axis=0).astype(F32)

    row = lax.broadcasted_iota(jnp.int32, (TILE, TILE), 0)
    col = lax.broadcasted_iota(jnp.int32, (TILE, TILE), 1)
    first, second = joined(ta_ref), joined(tb_ref)
    first_t, second_t = first.T, second.T
    folded = jnp.where(row < col, first + first_t, second + second_t)
    on_diagonal = jnp.broadcast_to(group % 7, (TILE, TILE)) == 0
    tt_ref[0:TILE, :] = jnp.where(on_diagonal, folded, first + second_t)
    own = jnp.sum(jnp.where(row == col, first, 0.0), axis=0, keepdims=True)
    targets = tt_ref[pl.ds(pl.multiple_of((y_lo * 2 + core) * MAIN, MAIN), MAIN), :]

    for i, c in enumerate(z_far):
        c.wait_recv()
        total = total + zb_ref[i]
    both = 2.0 * jax.nn.sigmoid(total)
    piece_ref[0:MAIN, :] = both[0:MAIN, :] - targets
    piece_ref[MAIN:ROWS, :] = both[MAIN:ROWS, :] - 2.0 * own

    spread = []
    for i, (dx, dy) in enumerate(OFFSETS):
        spread.append(copy(piece_ref, o_ref.at[core, mine], s3.at[i], r3.at[i], device(dx, dy)))
        spread[-1].start()
    own_out = copy(piece_ref, o_ref.at[core, mine], s4.at[15], r4.at[15], partner)
    own_out.start()
    o_ref[core, mine] = piece_ref[...]

    handed = []
    for i in reversed(range(15)):
        dx, dy = OFFSETS[i]
        p = place(-dx, -dy)
        copy(piece_ref, o_ref.at[core, p], s3.at[i], r3.at[i], device(dx, dy)).wait_recv()
        c = copy(o_ref.at[core, p], o_ref.at[core, p], s4.at[i], r4.at[i], partner)
        c.start()
        handed.append(c)
    for i in list(reversed(range(15))):
        dx, dy = OFFSETS[i]
        p = place(-dx, -dy)
        copy(o_ref.at[core, p], o_ref.at[other, p], s4.at[i], r4.at[i], partner).wait_recv()
    copy(piece_ref, o_ref.at[other, mine], s4.at[15], r4.at[15], partner).wait_recv()

    unpack(o_ref, s_ref)

    for c in t_near + t_far + t_plane + swaps + plane + z_near + z_far + spread + handed + [own_out]:
        c.wait_send()


def back_kernel(slot_ref, hw_ref, q_ref, k_ref, p_ref, s_ref, rb_ref, rr_ref, qg_ref, kg_ref, wg_ref, sb_ref, ds_ref):
    scale = DH ** (-0.5)
    w = slot_weights(slot_ref, hw_ref)
    chunk = 32
    zero = jnp.zeros((8, L), F32)

    def rows_of(i):
        return pl.ds(pl.multiple_of(i * chunk, chunk), chunk)

    def gather(i, carry):
        s = s_ref[rows_of(i), :]
        sb_ref[rows_of(i), :] = s.astype(BF16)
        out = []
        for layer in range(2):
            wide = jnp.concatenate([rb_ref[layer, rows_of(i), :]] * 4, axis=1)
            prod = s * wide
            acc = carry[layer]
            for t in range(chunk // 8):
                acc = acc + prod[t * 8 : (t + 1) * 8, :]
            out.append(acc)
        return tuple(out)

    sums = lax.fori_loop(0, L // chunk, gather, (zero, zero))
    for layer in range(2):
        h_row = jnp.sum(sums[layer], axis=0, keepdims=True)
        quad = jnp.sum(h_row * rr_ref[layer : layer + 1, :], axis=1, keepdims=True)
        h_col = jnp.dot(sb_ref[...], rb_ref[layer].astype(BF16), preferred_element_type=F32)
        ds_col = quad * (1.0 / (TOTAL * TOTAL)) - h_col * (1.0 / TOTAL)
        h_scaled = h_row * (1.0 / TOTAL)
        acc = zero
        for i in range(L // chunk):
            rows = slice(i * chunk, (i + 1) * chunk)
            s = s_ref[rows, :]
            probs = p_ref[layer, rows, :]
            wide = jnp.concatenate([ds_col[rows, :]] * 4, axis=1)
            dprobs = s + wide - h_scaled
            prod = probs * s
            for t in range(chunk // 8):
                acc = acc + prod[t * 8 : (t + 1) * 8, :]
            inner = jnp.sum(probs * dprobs, axis=1, keepdims=True)
            ds_ref[rows, :] = (probs * (dprobs - inner)).astype(BF16)
        wg_ref[layer : layer + 1, :] = jnp.sum(
            jnp.sum(acc, axis=0, keepdims=True), axis=1, keepdims=True
        ) - quad * (0.5 / TOTAL)
        factor = w[layer : layer + 1, :] * scale
        qg = jnp.dot(ds_ref[...], k_ref[layer], preferred_element_type=F32)
        qg_ref[layer] = (qg * factor).astype(BF16)
        kg = lax.dot_general(
            ds_ref[...], q_ref[layer], (((0,), (0,)), ((), ())), preferred_element_type=F32
        )
        kg_ref[layer] = (kg * factor).astype(BF16)


def vmem():
    return pl.BlockSpec(memory_space=pltpu.VMEM)


def smem():
    return pl.BlockSpec(memory_space=pltpu.SMEM)


def on_device(queries, keys, head_weight, slot_head, target):
    q = queries.reshape(2, L, DH)
    k = keys.reshape(2, L, DH)
    dma = pltpu.SemaphoreType.DMA
    probs, s_map, rb, rr = pl.pallas_call(
        exchange_kernel,
        out_shape=(
            jax.ShapeDtypeStruct((2, L, L), F32),
            jax.ShapeDtypeStruct((L, L), F32),
            jax.ShapeDtypeStruct((2, L, TILE), F32),
            jax.ShapeDtypeStruct((2, L), F32),
        ),
        in_specs=[smem(), vmem(), vmem(), vmem(), vmem()],
        out_specs=(vmem(), vmem(), vmem(), vmem()),
        scratch_shapes=[
            pltpu.VMEM((2, 16, ROWS, TILE), F32),
            pltpu.VMEM((16, ROWS, TILE), F32),
            pltpu.VMEM((15, ROWS, TILE), F32),
            pltpu.VMEM((15, ROWS, TILE), F32),
            pltpu.VMEM((2, ROWS, TILE), F32),
            pltpu.VMEM((3, ROWS, TILE), F32),
            pltpu.VMEM((3, ROWS, TILE), F32),
            pltpu.VMEM((16, 8, TILE), jnp.int32),
            pltpu.VMEM((16, 8, TILE), jnp.int32),
            pltpu.VMEM((2, 8, 8, TILE), jnp.int32),
            pltpu.VMEM((2, 8, 8, TILE), jnp.int32),
            pltpu.VMEM((TILE, TILE), F32),
            pltpu.VMEM((ROWS, TILE), F32),
            pltpu.VMEM((2, 16, ROWS, TILE), F32),
            dma((16,)), dma((16,)), dma((15,)), dma((15,)), dma((6,)), dma((6,)),
            dma((9,)), dma((9,)), dma((15,)), dma((15,)), dma((16,)), dma((16,)),
        ],
        compiler_params=pltpu.CompilerParams(collective_id=0, has_side_effects=True),
    )(slot_head, head_weight, target, q, k)
    qg, kg, wg = pl.pallas_call(
        back_kernel,
        out_shape=(
            jax.ShapeDtypeStruct((2, L, DH), BF16),
            jax.ShapeDtypeStruct((2, L, DH), BF16),
            jax.ShapeDtypeStruct((2, 1), F32),
        ),
        in_specs=[smem()] + [vmem()] * 7,
        out_specs=(vmem(), vmem(), vmem()),
        scratch_shapes=[pltpu.VMEM((L, L), BF16), pltpu.VMEM((L, L), BF16)],
    )(slot_head, head_weight, q, k, probs, s_map, rb, rr)
    return (qg.reshape(2, 1, L, DH), kg.reshape(2, 1, L, DH), wg)


def solution(mesh):
    placed = (
        P("layer", "head", None, None),
        P("layer", "head", None, None),
        P("layer", None),
        P("head"),
        P("head", None),
    )
    return jax.shard_map(
        on_device,
        mesh=mesh,
        in_specs=placed,
        out_specs=(P("layer", "head", None, None), P("layer", "head", None, None), P("layer", "head")),
        check_vma=False,
    )
```

time: 192 us -> 57.3 us (0.30)
  blocking collectives: 115 us -> 0 us
  Pallas kernels: 0 us -> 54.6 us
  other arithmetic: 23.5 us -> 0 us
  waiting for transfers between devices: 19.2 us -> 0 us
  between operations: 18.6 us -> 1.29 us
  local copies, waits for them, and re-layouts: 11.1 us -> 1.25 us
  matrix products: 3.76 us -> 0 us
    all_to_all x2 -> x0, blocking collectives: 80.8 us -> none  [the longest x1 71.3 us: sum_at_owner(): lax.all_to_all(tiles, axis, split_axis=0, concat_axis=0, tiled=True)]
    pallas_call x0 -> x2, Pallas kernels: none -> 54.6 us  [the longest x1 49.6 us: on_device(): pl.pallas_call(exchange_kernel, out_shape=(jax.ShapeDtypeStruct((2, L, L)...]
    all_gather x2 -> x0, blocking collectives: 34.1 us -> none  [stacked_from(): tiles = lax.all_gather(tiles, axes[k])]
    all_gather x1 -> x0, waiting for transfers between devices: 19.2 us -> none  [stacked_from(): tiles = lax.all_gather(tiles, axes[k])]
    reduce_sum x11 -> x0, other arithmetic: 16 us -> none  [the longest x1 6.83 us: pair_back(): wgrad = jnp.sum(error * feature)]
    dot_general x7 -> x0, matrix products: 3.76 us -> none  [the longest x2 1.7 us: pair_maps(): scores = jnp.dot(query, key.T, preferred_element_type=jnp.float32) * scale]
    another operation x3 -> x0, other arithmetic: 3.33 us -> none  [on_device(): return (jnp.stack(qlist), jnp.stack(klist), jnp.stack(wlist))]
    add x4 -> x0, local copies, waits for them, and re-layouts: 3.09 us -> none  [the longest x2 2.88 us: pair_back(): gmap - (u_vec[:, None] + v_vec[None, :]) / total]
  transfers between devices with their start and end apart: 1 -> 0, of which waited for: 1 -> 0; matrix products, arithmetic and copies ran while one was open for 0% -> 0% of each run, Pallas kernels for 0% -> 0%
where the time goes in v1:
time: 57.3 us; the launch traced here: 57.1 us
  Pallas kernels  54.6 us (95%)
  between operations  1.29 us (2%)
  local copies, waits for them, and re-layouts  1.25 us (2%)
    pallas_call x1, Pallas kernels, on_device(): pl.pallas_call(exchange_kernel, out_shape=(jax.ShapeDtypeStruct((2, L, L)...  49.6 us
    pallas_call x1, Pallas kernels, on_device(): pl.pallas_call(back_kernel, out_shape=(jax.ShapeDtypeStruct((2, L, DH), B...  4.99 us
    unnamed x1, local copies, waits for them, and re-layouts  1.25 us

profile of v1, /device:TPU:1, one launch (start us, length us, event | category | flops | bytes accessed | tf_op | source)
XLA Modules:
  0.0 57.1 jit_solution(17929721153543366335)
XLA Ops:
  1.3 49.6 %shard_map.76 = (f32[2,512,512]{2,1,0:T(8,128)}, f32[512,512]{1,0:T(8,128)}, f32[2,512,128]{2,1,0:T(8,128)}, f32[2,512]{1,0:T(2,128)}) custom-call(s32[1]{0:T(128)S(6)} %copy.11.slot_ref, f32[2,40]{1,0:T(2,128)} %hw_ref.3, s32[8,512]{1,0:T(8,128)} %target_ref.1, bf16[2,512,128]{2,1,0:T(8,128)(2,1)} %bitcast.8, bf16[2,512,128]{2,1,0:T(8,128)(2,1)} %bitcast.10), custom_call_target="tpu_custom_call" | custom-call | tf_op jit(solution)/shard_map/pallas_call | solution.py:352
  50.9 5.0 %shard_map.77 = (bf16[2,512,128]{2,1,0:T(8,128)(2,1)}, bf16[2,512,128]{2,1,0:T(8,128)(2,1)}, f32[2,1]{1,0:T(2,128)}) custom-call(s32[1]{0:T(128)S(6)} %copy.11.slot_ref, f32[2,40]{1,0:T(2,128)} %hw_ref.3, bf16[2,512,128]{2,1,0:T(8,128)(2,1)} %bitcast.9, bf16[2,512,128]{2,1,0:T(8,128)(2,1)} %bitcast.11, f32[2,512,512]{2,1,0:T(8,128)} %get-tuple-element.10.p_ref, ...), custom_call_target="tpu_custom_call" | custom-call | tf_op jit(solution)/shard_map/pallas_call | solution.py:382
  55.8 1.2 %copy.10 = f32[2,1]{0,1:T(1,128)} copy(f32[2,1]{1,0:T(2,128)} %get-tuple-element.19) | data formatting | bytes 16

commit v2 on v1

v2 whole, which is shorter than its diff:
```python
import jax
import jax.numpy as jnp
from jax import lax
from jax.experimental import pallas as pl
from jax.experimental.pallas import tpu as pltpu
from jax.sharding import PartitionSpec as P

MESH = pl.DeviceIdType.MESH
F32 = jnp.float32
BF16 = jnp.bfloat16
L = 512
DH = 128
TILE = 128
TOTAL = 2.0 * L
OFF = {1: (0, 1), 2: (0, 2), 3: (1, 3), 4: (3, 0), 5: (2, 1), 6: (3, 2)}
DIAG = {0: (0, 1), 7: (3, 2)}
KEEP = (0, 0, 0, 1, 1, 0, 1, 1)
MIRROR = (1, 0, 5, 4, 2, 3, 7, 6)
MIRRORED = (1, 0, 4, 5, 3, 2, 7, 6)
ROWS = 32
OFFSETS = sorted(
    ((dx, dy) for dx in range(4) for dy in range(4) if dx or dy),
    key=lambda o: -(min(o[0], 4 - o[0]) + min(o[1], 4 - o[1])),
)


def pick(index, table):
    value = jnp.int32(table[0])
    for k in range(1, len(table)):
        value = jnp.where(index == k, jnp.int32(table[k]), value)
    return value


def slot_weights(slot_ref, hw_ref):
    hw = hw_ref[...]
    lane = lax.broadcasted_iota(jnp.int32, hw.shape, 1)
    return jnp.sum(jnp.where(lane == slot_ref[0], hw, 0.0), axis=1, keepdims=True)


def forward(w, qk_ref, ready, sc_ref, p_ref, rb_ref, rr_ref, x_ref, e_ref):
    scale = DH ** (-0.5)
    chunk = 32
    sums = []
    for layer in range(2):
        ready(layer)
        sc_ref[...] = lax.dot_general(
            qk_ref[layer, 0], qk_ref[layer, 1], (((1,), (1,)), ((), ())), preferred_element_type=F32
        )

        def body(i, csum, layer=layer):
            rows = pl.ds(pl.multiple_of(i * chunk, chunk), chunk)
            scores = sc_ref[rows, :]
            highest = jnp.max(scores, axis=1, keepdims=True)
            expo = jnp.exp((scores - highest) * scale)
            probs = expo * (1.0 / jnp.sum(expo, axis=1, keepdims=True))
            p_ref[layer, rows, :] = probs
            for t in range(chunk // 8):
                csum = csum + probs[t * 8 : (t + 1) * 8, :]
            return csum

        csum = lax.fori_loop(0, L // chunk, body, jnp.zeros((8, L), F32), unroll=4)
        rowsum = 1.0 + jnp.sum(csum, axis=0, keepdims=True)
        rr_ref[layer : layer + 1, :] = rowsum
        for t in range(4):
            wide = jnp.broadcast_to(rowsum[:, t * TILE : (t + 1) * TILE], (TILE, TILE))
            rb_ref[layer, t * TILE : (t + 1) * TILE, :] = wide.T
        sums.append(rowsum * (w[layer : layer + 1, 0:1] / TOTAL))

    def cut(t):
        return slice(t * TILE, (t + 1) * TILE)

    def half(a, b):
        return w[0:1, :] * p_ref[0, cut(a), cut(b)] + w[1:2, :] * p_ref[1, cut(a), cut(b)]

    def block(a, b):
        outer = rb_ref[0, cut(a), :] * sums[0][:, cut(b)] + rb_ref[1, cut(a), :] * sums[1][:, cut(b)]
        return half(a, b) + half(b, a).T - outer

    row = lax.broadcasted_iota(jnp.int32, (TILE, TILE), 0)
    col = lax.broadcasted_iota(jnp.int32, (TILE, TILE), 1)
    for g in range(8):
        if g in OFF:
            full = block(*OFF[g])
        else:
            upper = block(DIAG[g][0], DIAG[g][0])
            full = jnp.where(row < col, upper, block(DIAG[g][1], DIAG[g][1]))
            extra = jnp.sum(jnp.where(row == col, upper, 0.0), axis=0, keepdims=True)
            e_ref[g // 7] = jnp.broadcast_to(extra, (8, TILE))
        for part in range(4):
            x_ref[part % 2, 2 * g + part // 2] = full[part * ROWS : (part + 1) * ROWS, :]


def unpack(o_ref, eo_ref, s_ref):
    row = lax.broadcasted_iota(jnp.int32, (TILE, TILE), 0)
    col = lax.broadcasted_iota(jnp.int32, (TILE, TILE), 1)

    def cut(t):
        return slice(t * TILE, (t + 1) * TILE)

    for g in range(8):
        full = jnp.concatenate([o_ref[part % 2, 2 * g + part // 2] for part in range(4)], axis=0)
        if g in OFF:
            a, b = OFF[g]
            s_ref[cut(a), cut(b)] = full
            s_ref[cut(b), cut(a)] = full.T
        else:
            a, b = DIAG[g]
            turned = full.T
            diagonal = eo_ref[g // 7, 0:1, :]
            upper = jnp.where(row < col, full, jnp.where(row == col, diagonal, turned))
            s_ref[cut(a), cut(a)] = upper
            s_ref[cut(b), cut(b)] = jnp.where(row < col, turned, full)


def exchange_kernel(
    slot_ref, hw_hbm, target_hbm, q_hbm, k_hbm,
    p_ref, s_ref, rb_ref, rr_ref, w_ref, qk_ref, qt_ref,
    hw_ref, target_ref, sc_ref, x_ref, a_ref, y_ref, b_ref, z_ref, zn_ref, zf_ref,
    t_ref, to_ref, ta_ref, tb_ref, tt_ref, piece_ref, o_ref,
    e_ref, ey_ref, eb_ref, ez_ref, en_ref, ef_ref, ep_ref, eo_ref,
    sin, s0, r0, s1, r1, sz, rz, st, rt, s3, r3, s4, r4, es, er,
):
    loads = [
        pltpu.make_async_copy(q_hbm.at[0], qk_ref.at[0, 0], sin.at[0]),
        pltpu.make_async_copy(k_hbm.at[0], qk_ref.at[0, 1], sin.at[0]),
        pltpu.make_async_copy(hw_hbm, hw_ref, sin.at[2]),
        pltpu.make_async_copy(q_hbm.at[1], qk_ref.at[1, 0], sin.at[1]),
        pltpu.make_async_copy(k_hbm.at[1], qk_ref.at[1, 1], sin.at[1]),
        pltpu.make_async_copy(target_hbm, target_ref, sin.at[3]),
    ]
    for c in loads:
        c.start()
    layer_pos = lax.axis_index("layer")
    head_pos = lax.axis_index("head")
    x = layer_pos % 4
    y_lo = layer_pos // 4
    core = head_pos % 2
    z = (head_pos // 2) % 16
    y_hi = head_pos // 32
    y = y_hi * 2 + y_lo
    group = y_hi * 4 + x
    other = 1 - core
    mine = group * 2 + y_lo

    def device(dx=0, dy=0, dz=0, flip=False):
        nx = (x + dx) % 4
        ny = (y + dy) % 4
        nz = (z + dz) % 16
        nc = other if flip else core
        return {"layer": (ny % 2) * 4 + nx, "head": (ny // 2) * 32 + nz * 2 + nc}

    def place(dx, dy):
        nx = (x + dx) % 4
        ny = (y + dy) % 4
        return ((ny // 2) * 4 + nx) * 2 + ny % 2

    def in_group(g, c):
        return {"layer": y_lo * 4 + g % 4, "head": (g // 4) * 32 + z * 2 + c}

    partner = device(flip=True)
    sent_to = pick(group, MIRROR)
    got_from = pick(group, MIRRORED)

    barrier = pltpu.get_barrier_semaphore()
    greeted = [device(dz=d) for d in (8, 5, -5, 2, -2, 1, -1)]
    greeted += [device(dx, dy) for dx, dy in OFFSETS]
    greeted += [partner, in_group(sent_to, other), in_group(got_from, other)]
    for d in greeted:
        pl.semaphore_signal(barrier, inc=1, device_id=d, device_id_type=MESH)

    def ready(layer):
        pltpu.make_async_copy(qk_ref.at[layer], qk_ref.at[layer], sin.at[layer]).wait()
        if layer == 0:
            loads[2].wait()
            w = slot_weights(slot_ref, hw_ref)
            w_ref[...] = jnp.broadcast_to(w, (2, TILE))

    forward(w_ref, qk_ref, ready, sc_ref, p_ref, rb_ref, rr_ref, x_ref, e_ref)
    loads[5].wait()
    pl.semaphore_wait(barrier, len(greeted))

    def copy(src, dst, ssem, rsem, dev):
        return pltpu.make_async_remote_copy(
            src_ref=src, dst_ref=dst, send_sem=ssem, recv_sem=rsem, device_id=dev, device_id_type=MESH
        )

    def arrived(ref, rsem):
        copy(ref, ref, s0, rsem, partner).wait_recv()

    def left(ref, ssem):
        copy(ref, ref, ssem, r1, partner).wait_send()

    tile = target_ref.at[:, pl.ds(pl.multiple_of(x * TILE, TILE), TILE)]
    for d, slot in ((1, 6), (-1, 8), (2, 5), (-2, 9)):
        copy(tile, t_ref.at[slot], st.at[0], rt.at[0], device(dz=d)).start()
    copy(tile, t_ref.at[15], st.at[0], rt.at[1], device(dz=8)).start()
    t_ref[7] = target_ref[:, pl.ds(pl.multiple_of(x * TILE, TILE), TILE)]

    order = OFFSETS + [(0, 0)]
    for i, (dx, dy) in enumerate(order):
        copy(x_ref.at[other, place(dx, dy)], a_ref.at[pl.ds(i * ROWS, ROWS)], s0, r0.at[i // 4], partner).start()
    copy(e_ref.at[other], a_ref.at[pl.ds(16 * ROWS, 8)], s0, r0.at[3], partner).start()

    for i, (dx, dy) in enumerate(order):
        if i % 4 == 0:
            arrived(a_ref.at[pl.ds(i * ROWS, 4 * ROWS + (8 if i == 12 else 0))], r0.at[i // 4])
        summed = x_ref[core, place(dx, dy)] + a_ref[i * ROWS : (i + 1) * ROWS, :]
        if i < 15:
            y_ref[i] = summed
            copy(y_ref.at[i], b_ref.at[i], s1, r1, device(dx, dy)).start()
        else:
            total = summed

    ey_ref[...] = e_ref[core] + a_ref[16 * ROWS : 16 * ROWS + 8, :]
    owner = mine == core * 14
    owner_of_diagonal = {"layer": core * 3, "head": core * 33 + z * 2}

    @pl.when(jnp.logical_not(owner))
    def _():
        copy(ey_ref, eb_ref.at[mine], es.at[0], er.at[0], owner_of_diagonal).start()

    arrived(t_ref.at[pl.ds(5, 4)], rt.at[0])
    copy(t_ref.at[pl.ds(5, 5)], t_ref.at[pl.ds(0, 5)], st.at[0], rt.at[1], device(dz=5)).start()
    copy(t_ref.at[pl.ds(5, 5)], t_ref.at[pl.ds(10, 5)], st.at[0], rt.at[1], device(dz=-5)).start()

    arrived(b_ref, r1)
    for i in range(15):
        total = total + b_ref[i]
    z_ref[0] = total
    near = (1, -1, 2, -2)
    for i, d in enumerate(near):
        copy(z_ref.at[0], zn_ref.at[i], sz.at[0], rz.at[0], device(dz=d)).start()
    copy(z_ref.at[0], zn_ref.at[4], sz.at[0], rz.at[2], device(dz=8)).start()

    @pl.when(owner)
    def _():
        eb_ref[mine] = ey_ref[...]
        arrived(eb_ref.at[pl.ds(0, 15)], er.at[0])
        acc = eb_ref[0]
        for i in range(1, 16):
            acc = acc + eb_ref[i]
        ez_ref[0] = acc
        for i, d in enumerate(near):
            copy(ez_ref.at[0], en_ref.at[i], es.at[1], er.at[1], device(dz=d)).start()
        copy(ez_ref.at[0], en_ref.at[4], es.at[1], er.at[3], device(dz=8)).start()

    arrived(t_ref.at[pl.ds(0, 11)], rt.at[1])
    for slot in range(16):
        to_ref[(z + slot + 9) % 16] = t_ref[slot]
    keep = pick(group, KEEP)
    kept = to_ref.at[pl.ds(keep * 8, 8)]
    given = to_ref.at[pl.ds((1 - keep) * 8, 8)]
    copy(kept, ta_ref.at[core], st.at[1], rt.at[2], partner).start()
    copy(given, tb_ref.at[core], st.at[2], rt.at[3], in_group(sent_to, core)).start()
    copy(given, tb_ref.at[core], st.at[2], rt.at[3], in_group(sent_to, other)).start()
    ta_ref[core] = to_ref[pl.ds(keep * 8, 8)]
    arrived(zn_ref.at[pl.ds(0, 4)], rz.at[0])
    for i in range(4):
        total = total + zn_ref[i]
    z_ref[1] = total
    for i, d in enumerate((5, -5)):
        copy(z_ref.at[1], zf_ref.at[i], sz.at[1], rz.at[1], device(dz=d)).start()

    @pl.when(owner)
    def _():
        arrived(en_ref.at[pl.ds(0, 4)], er.at[1])
        acc = ez_ref[0]
        for i in range(4):
            acc = acc + en_ref[i]
        ez_ref[1] = acc
        for i, d in enumerate((5, -5)):
            copy(ez_ref.at[1], ef_ref.at[i], es.at[2], er.at[2], device(dz=d)).start()

    for layer in range(2):
        qt_ref[layer] = qk_ref[layer, 0].astype(F32).T.astype(BF16)

    arrived(ta_ref.at[other], rt.at[2])
    arrived(tb_ref, rt.at[3])

    def joined(ref):
        return jnp.concatenate([ref[t % 2, t // 2] for t in range(16)], axis=0).astype(F32)

    row = lax.broadcasted_iota(jnp.int32, (TILE, TILE), 0)
    col = lax.broadcasted_iota(jnp.int32, (TILE, TILE), 1)
    first, second = joined(ta_ref), joined(tb_ref)
    first_t, second_t = first.T, second.T
    folded = jnp.where(row < col, first + first_t, second + second_t)
    on_diagonal = jnp.broadcast_to(group % 7, (TILE, TILE)) == 0
    tt_ref[...] = jnp.where(on_diagonal, folded, first + second_t)
    own = jnp.sum(jnp.where(row == col, first, 0.0), axis=0, keepdims=True)
    targets = tt_ref[pl.ds(pl.multiple_of((y_lo * 2 + core) * ROWS, ROWS), ROWS), :]

    arrived(zf_ref, rz.at[1])
    arrived(zn_ref.at[4], rz.at[2])
    total = total + zf_ref[0] + zf_ref[1] + zn_ref[4]
    piece_ref[...] = 2.0 * jax.nn.sigmoid(total) - targets
    for i, (dx, dy) in enumerate(OFFSETS):
        copy(piece_ref, o_ref.at[core, mine], s3, r3.at[i], device(dx, dy)).start()
    copy(piece_ref, o_ref.at[core, mine], s4, r4, partner).start()
    o_ref[core, mine] = piece_ref[...]

    @pl.when(owner)
    def _():
        arrived(ef_ref, er.at[2])
        arrived(en_ref.at[4], er.at[3])
        acc = ez_ref[1] + ef_ref[0] + ef_ref[1] + en_ref[4]
        ep_ref[...] = 2.0 * jax.nn.sigmoid(acc) - 2.0 * own
        for dx, dy in OFFSETS:
            copy(ep_ref, eo_ref.at[core], es.at[3], er.at[4], device(dx, dy)).start()
        copy(ep_ref, eo_ref.at[core], es.at[4], er.at[5], partner).start()
        eo_ref[core] = ep_ref[...]

    for i in reversed(range(15)):
        dx, dy = OFFSETS[i]
        piece = o_ref.at[core, place(-dx, -dy)]
        arrived(piece, r3.at[i])
        copy(piece, piece, s4, r4, partner).start()

    @pl.when(jnp.logical_not(owner))
    def _():
        arrived(eo_ref.at[core], er.at[4])
        copy(eo_ref.at[core], eo_ref.at[core], es.at[4], er.at[5], partner).start()

    arrived(o_ref.at[other], r4)
    arrived(eo_ref.at[other], er.at[5])
    unpack(o_ref, eo_ref, s_ref)

    left(a_ref, s0)
    left(y_ref, s1)
    left(zn_ref, sz.at[0])
    left(zf_ref, sz.at[1])
    left(t_ref.at[pl.ds(0, 15)], st.at[0])
    left(ta_ref.at[core], st.at[1])
    left(tb_ref, st.at[2])
    left(b_ref, s3)
    left(o_ref.at[core], s4)
    left(ep_ref, es.at[4])

    @pl.when(owner)
    def _():
        left(en_ref, es.at[1])
        left(ef_ref, es.at[2])
        left(eb_ref.at[pl.ds(0, 15)], es.at[3])

    @pl.when(jnp.logical_not(owner))
    def _():
        left(ey_ref, es.at[0])


def back_kernel(w_ref, qt_ref, qk_ref, p_ref, s_ref, rb_ref, rr_ref, qg_hbm, kg_hbm, wg_ref, d_ref, ds_ref, qg_ref, kg_ref, sems):
    scale = DH ** (-0.5)
    chunk = 32
    zero = jnp.zeros((8, L), F32)

    def gather(i, carry):
        rows = pl.ds(pl.multiple_of(i * chunk, chunk), chunk)
        s = s_ref[rows, :]
        out = []
        for layer in range(2):
            wide = jnp.concatenate([rb_ref[layer, rows, :]] * 4, axis=1)
            prod = s * wide
            acc = carry[layer]
            for t in range(chunk // 8):
                acc = acc + prod[t * 8 : (t + 1) * 8, :]
            out.append(acc)
        return tuple(out)

    sums = lax.fori_loop(0, L // chunk, gather, (zero, zero), unroll=2)
    grads = []
    stores = []
    for layer in range(2):
        h_row = jnp.sum(sums[layer], axis=0, keepdims=True)
        quad = jnp.sum(h_row * rr_ref[layer : layer + 1, :], axis=1, keepdims=True)
        h_scaled = h_row * (1.0 / TOTAL)
        d_row = quad * (1.0 / (TOTAL * TOTAL)) - h_scaled
        for t in range(4):
            wide = jnp.broadcast_to(d_row[:, t * TILE : (t + 1) * TILE], (TILE, TILE))
            d_ref[layer, t * TILE : (t + 1) * TILE, :] = wide.T
        acc = zero
        for i in range(L // chunk):
            rows = slice(i * chunk, (i + 1) * chunk)
            s = s_ref[rows, :]
            probs = p_ref[layer, rows, :]
            wide = jnp.concatenate([d_ref[layer, rows, :]] * 4, axis=1)
            dprobs = s + wide - h_scaled
            prod = probs * s
            for t in range(chunk // 8):
                acc = acc + prod[t * 8 : (t + 1) * 8, :]
            inner = jnp.sum(probs * dprobs, axis=1, keepdims=True)
            ds_ref[layer, rows, :] = (probs * (dprobs - inner)).astype(BF16)
        grads.append(jnp.sum(jnp.sum(acc, axis=0, keepdims=True), axis=1, keepdims=True) - quad * (0.5 / TOTAL))
        factor = w_ref[layer : layer + 1, :] * scale
        qg = jnp.dot(ds_ref[layer], qk_ref[layer, 1], preferred_element_type=F32)
        qg_ref[layer] = (qg * factor).astype(BF16)
        stores.append(pltpu.make_async_copy(qg_ref.at[layer], qg_hbm.at[layer], sems.at[2 * layer]))
        stores[-1].start()
        kg = jnp.dot(qt_ref[layer], ds_ref[layer], preferred_element_type=F32)
        kg_ref[layer] = (kg.T * factor).astype(BF16)
        stores.append(pltpu.make_async_copy(kg_ref.at[layer], kg_hbm.at[layer], sems.at[2 * layer + 1]))
        stores[-1].start()
    lane = lax.broadcasted_iota(jnp.int32, (1, 2), 1)
    wg_ref[...] = jnp.where(lane == 0, grads[0], grads[1])
    for c in stores:
        c.wait()


def vmem():
    return pl.BlockSpec(memory_space=pltpu.VMEM)


def smem():
    return pl.BlockSpec(memory_space=pltpu.SMEM)


def hbm():
    return pl.BlockSpec(memory_space=pltpu.HBM)


def on_device(queries, keys, head_weight, slot_head, target):
    q = queries.reshape(2, L, DH)
    k = keys.reshape(2, L, DH)
    dma = pltpu.SemaphoreType.DMA
    probs, s_map, rb, rr, w, qk, q_turned = pl.pallas_call(
        exchange_kernel,
        out_shape=(
            pltpu.VMEM((2, L, L), F32),
            pltpu.VMEM((L, L), F32),
            pltpu.VMEM((2, L, TILE), F32),
            pltpu.VMEM((2, L), F32),
            pltpu.VMEM((2, TILE), F32),
            pltpu.VMEM((2, 2, L, DH), BF16),
            pltpu.VMEM((2, DH, L), BF16),
        ),
        in_specs=[smem()] + [hbm()] * 4,
        out_specs=(vmem(),) * 7,
        scratch_shapes=[
            pltpu.VMEM((2, 40), F32),
            pltpu.VMEM((8, L), jnp.int32),
            pltpu.VMEM((L, L), F32),
            pltpu.VMEM((2, 16, ROWS, TILE), F32),
            pltpu.VMEM((16 * ROWS + 8, TILE), F32),
            pltpu.VMEM((15, ROWS, TILE), F32),
            pltpu.VMEM((15, ROWS, TILE), F32),
            pltpu.VMEM((2, ROWS, TILE), F32),
            pltpu.VMEM((5, ROWS, TILE), F32),
            pltpu.VMEM((2, ROWS, TILE), F32),
            pltpu.VMEM((16, 8, TILE), jnp.int32),
            pltpu.VMEM((16, 8, TILE), jnp.int32),
            pltpu.VMEM((2, 8, 8, TILE), jnp.int32),
            pltpu.VMEM((2, 8, 8, TILE), jnp.int32),
            pltpu.VMEM((TILE, TILE), F32),
            pltpu.VMEM((ROWS, TILE), F32),
            pltpu.VMEM((2, 16, ROWS, TILE), F32),
            pltpu.VMEM((2, 8, TILE), F32),
            pltpu.VMEM((8, TILE), F32),
            pltpu.VMEM((16, 8, TILE), F32),
            pltpu.VMEM((2, 8, TILE), F32),
            pltpu.VMEM((5, 8, TILE), F32),
            pltpu.VMEM((2, 8, TILE), F32),
            pltpu.VMEM((8, TILE), F32),
            pltpu.VMEM((2, 8, TILE), F32),
            dma((4,)), dma, dma((4,)), dma, dma, dma((2,)), dma((3,)), dma((3,)), dma((4,)),
            dma, dma((15,)), dma, dma, dma((5,)), dma((6,)),
        ],
        compiler_params=pltpu.CompilerParams(collective_id=0, has_side_effects=True, vmem_limit_bytes=16 << 20),
    )(slot_head, *[pltpu.with_memory_space_constraint(v, pltpu.HBM) for v in (head_weight, target, q, k)])
    qg, kg, wg = pl.pallas_call(
        back_kernel,
        out_shape=(
            jax.ShapeDtypeStruct((2, L, DH), BF16),
            jax.ShapeDtypeStruct((2, L, DH), BF16),
            jax.ShapeDtypeStruct((1, 2), F32),
        ),
        in_specs=[vmem()] * 7,
        out_specs=(hbm(), hbm(), vmem()),
        scratch_shapes=[
            pltpu.VMEM((2, L, TILE), F32),
            pltpu.VMEM((2, L, L), BF16),
            pltpu.VMEM((2, L, DH), BF16),
            pltpu.VMEM((2, L, DH), BF16),
            pltpu.SemaphoreType.DMA((4,)),
        ],
        compiler_params=pltpu.CompilerParams(vmem_limit_bytes=16 << 20),
    )(w, q_turned, qk, probs, s_map, rb, rr)
    return (qg.reshape(2, 1, L, DH), kg.reshape(2, 1, L, DH), wg.reshape(2, 1))


def solution(mesh):
    placed = (
        P("layer", "head", None, None),
        P("layer", "head", None, None),
        P("layer", None),
        P("head"),
        P("head", None),
    )
    return jax.shard_map(
        on_device,
        mesh=mesh,
        in_specs=placed,
        out_specs=(P("layer", "head", None, None), P("layer", "head", None, None), P("layer", "head")),
        check_vma=False,
    )
```

time: 57.3 us -> 45.3 us (0.79)
  Pallas kernels: 54.6 us -> 43.9 us
  local copies, waits for them, and re-layouts: 1.25 us -> 0 us
    pallas_call x1, Pallas kernels: 49.6 us -> 41.2 us  [on_device(): pl.pallas_call(exchange_kernel, out_shape=(pltpu.VMEM((2, L, L), F32), pl...]
    pallas_call x1, Pallas kernels: 4.99 us -> 2.73 us  [on_device(): pl.pallas_call(back_kernel, out_shape=(jax.ShapeDtypeStruct((2, L, DH), B...]
    unnamed x1 -> x0, local copies, waits for them, and re-layouts: 1.25 us -> none
where the time goes in v2:
time: 45.3 us; the launch traced here: 45.2 us
  Pallas kernels  43.9 us (97%)
  between operations  1.29 us (3%)
    pallas_call x1, Pallas kernels, on_device(): pl.pallas_call(exchange_kernel, out_shape=(pltpu.VMEM((2, L, L), F32), pl...  41.2 us
    pallas_call x1, Pallas kernels, on_device(): pl.pallas_call(back_kernel, out_shape=(jax.ShapeDtypeStruct((2, L, DH), B...  2.73 us

profile of v2, /device:TPU:1, one launch (start us, length us, event | category | flops | bytes accessed | tf_op | source)
XLA Modules:
  0.0 45.2 jit_solution(10166441599948231281)
XLA Ops:
  1.3 41.2 %shard_map.76 = (f32[2,512,512]{2,1,0:T(8,128)S(1)}, f32[512,512]{1,0:T(8,128)S(1)}, f32[2,512,128]{2,1,0:T(8,128)S(1)}, f32[2,512]{1,0:T(2,128)S(1)}, f32[2,128...) custom-call(s32[1]{0:T(128)S(6)} %copy.10.slot_ref, f32[2,40]{1,0:T(2,128)} %hw_hbm.1, ...), custom_call_target="tpu_custom_call" | custom-call | tf_op jit(solution)/shard_map/pallas_call | solution.py:423
  42.5 2.7 %shard_map.77 = (bf16[2,512,128]{2,1,0:T(8,128)(2,1)}, bf16[2,512,128]{2,1,0:T(8,128)(2,1)}, f32[1,2]{1,0:T(1,128)}) custom-call(f32[2,128]{1,0:T(2,128)S(1)} %get-tuple-element.13.w_ref, bf16[2,128,512]{2,1,0:T(8,128)(2,1)S(1)} %get-tuple-element.14.qt_ref, bf16[2,2,512,128]{3,2,1,0:T(8,128)(2,1)S(1)} %get-tuple-element.15.qk_ref, ...), custom_call_target="tpu_custom_call" | custom-call | tf_op jit(solution)/shard_map/pallas_call | solution.py:467

commit v3 on v2

--- a/solution.py
+++ b/solution.py
@@ -23,6 +23,8 @@
     key=lambda o: -(min(o[0], 4 - o[0]) + min(o[1], 4 - o[1])),
 )
 
+GROUPS = (0,) * 5 + (1,) * 3 + (2,) * 3 + (3,) * 4
+
 
 def pick(index, table):
     value = jnp.int32(table[0])
@@ -58,7 +60,7 @@
                 csum = csum + probs[t * 8 : (t + 1) * 8, :]
             return csum
 
-        csum = lax.fori_loop(0, L // chunk, body, jnp.zeros((8, L), F32), unroll=4)
+        csum = lax.fori_loop(0, L // chunk, body, jnp.zeros((8, L), F32), unroll=16)
         rowsum = 1.0 + jnp.sum(csum, axis=0, keepdims=True)
         rr_ref[layer : layer + 1, :] = rowsum
         for t in range(4):
@@ -116,9 +118,9 @@
     slot_ref, hw_hbm, target_hbm, q_hbm, k_hbm,
     p_ref, s_ref, rb_ref, rr_ref, w_ref, qk_ref, qt_ref,
     hw_ref, target_ref, sc_ref, x_ref, a_ref, y_ref, b_ref, z_ref, zn_ref, zf_ref,
-    t_ref, to_ref, ta_ref, tb_ref, tt_ref, piece_ref, o_ref,
+    tn_ref, t_ref, to_ref, ta_ref, tb_ref, tt_ref, piece_ref, o_ref,
     e_ref, ey_ref, eb_ref, ez_ref, en_ref, ef_ref, ep_ref, eo_ref,
-    sin, s0, r0, s1, r1, sz, rz, st, rt, s3, r3, s4, r4, es, er,
+    sin, s0, r0, s1, r1, sz, rz, st, rt, s3, r3, s4, r4, es, er, relay,
 ):
     loads = [
         pltpu.make_async_copy(q_hbm.at[0], qk_ref.at[0, 0], sin.at[0]),
@@ -141,11 +143,12 @@
     group = y_hi * 4 + x
     other = 1 - core
     mine = group * 2 + y_lo
+    sign = 1 - 2 * core
 
     def device(dx=0, dy=0, dz=0, flip=False):
         nx = (x + dx) % 4
         ny = (y + dy) % 4
-        nz = (z + dz) % 16
+        nz = (z + sign * dz + 16) % 16
         nc = other if flip else core
         return {"layer": (ny % 2) * 4 + nx, "head": (ny // 2) * 32 + nz * 2 + nc}
 
@@ -162,8 +165,8 @@
     got_from = pick(group, MIRRORED)
 
     barrier = pltpu.get_barrier_semaphore()
-    greeted = [device(dz=d) for d in (8, 5, -5, 2, -2, 1, -1)]
-    greeted += [device(dx, dy) for dx, dy in OFFSETS]
+    greeted = [device(dx, dy) for dx, dy in OFFSETS]
+    greeted += [device(dz=d) for d in (3, -3, 2, -2, 1, -1)]
     greeted += [partner, in_group(sent_to, other), in_group(got_from, other)]
     for d in greeted:
         pl.semaphore_signal(barrier, inc=1, device_id=d, device_id_type=MESH)
@@ -191,19 +194,27 @@
         copy(ref, ref, ssem, r1, partner).wait_send()
 
     tile = target_ref.at[:, pl.ds(pl.multiple_of(x * TILE, TILE), TILE)]
-    for d, slot in ((1, 6), (-1, 8), (2, 5), (-2, 9)):
-        copy(tile, t_ref.at[slot], st.at[0], rt.at[0], device(dz=d)).start()
-    copy(tile, t_ref.at[15], st.at[0], rt.at[1], device(dz=8)).start()
-    t_ref[7] = target_ref[:, pl.ds(pl.multiple_of(x * TILE, TILE), TILE)]
+    for d, slot in ((1, 1), (-1, 3), (2, 0), (-2, 4), (-3, 5)):
+        copy(tile, tn_ref.at[slot], st.at[0], rt.at[0], device(dz=d)).start()
+    tn_ref[2] = target_ref[:, pl.ds(pl.multiple_of(x * TILE, TILE), TILE)]
 
     order = OFFSETS + [(0, 0)]
+    copy(e_ref.at[other], a_ref.at[pl.ds(16 * ROWS, 8)], s0, r0.at[0], partner).start()
     for i, (dx, dy) in enumerate(order):
-        copy(x_ref.at[other, place(dx, dy)], a_ref.at[pl.ds(i * ROWS, ROWS)], s0, r0.at[i // 4], partner).start()
-    copy(e_ref.at[other], a_ref.at[pl.ds(16 * ROWS, 8)], s0, r0.at[3], partner).start()
+        copy(x_ref.at[other, place(dx, dy)], a_ref.at[pl.ds(i * ROWS, ROWS)], s0, r0.at[1 + i // 4], partner).start()
+
+    arrived(a_ref.at[pl.ds(16 * ROWS, 8)], r0.at[0])
+    ey_ref[...] = e_ref[core] + a_ref[16 * ROWS : 16 * ROWS + 8, :]
+    owner = mine == core * 14
+    owner_of_diagonal = {"layer": core * 3, "head": core * 33 + z * 2}
+
+    @pl.when(jnp.logical_not(owner))
+    def _():
+        copy(ey_ref, eb_ref.at[mine], es.at[0], er.at[0], owner_of_diagonal).start()
 
     for i, (dx, dy) in enumerate(order):
         if i % 4 == 0:
-            arrived(a_ref.at[pl.ds(i * ROWS, 4 * ROWS + (8 if i == 12 else 0))], r0.at[i // 4])
+            arrived(a_ref.at[pl.ds(i * ROWS, 4 * ROWS)], r0.at[1 + i // 4])
         summed = x_ref[core, place(dx, dy)] + a_ref[i * ROWS : (i + 1) * ROWS, :]
         if i < 15:
             y_ref[i] = summed
@@ -211,17 +222,10 @@
         else:
             total = summed
 
-    ey_ref[...] = e_ref[core] + a_ref[16 * ROWS : 16 * ROWS + 8, :]
-    owner = mine == core * 14
-    owner_of_diagonal = {"layer": core * 3, "head": core * 33 + z * 2}
-
-    @pl.when(jnp.logical_not(owner))
-    def _():
-        copy(ey_ref, eb_ref.at[mine], es.at[0], er.at[0], owner_of_diagonal).start()
-
-    arrived(t_ref.at[pl.ds(5, 4)], rt.at[0])
-    copy(t_ref.at[pl.ds(5, 5)], t_ref.at[pl.ds(0, 5)], st.at[0], rt.at[1], device(dz=5)).start()
-    copy(t_ref.at[pl.ds(5, 5)], t_ref.at[pl.ds(10, 5)], st.at[0], rt.at[1], device(dz=-5)).start()
+    arrived(t_ref.at[pl.ds(0, 5)], rt.at[0])
+    pl.semaphore_signal(relay, inc=1, device_id=device(dz=-5), device_id_type=MESH)
+    copy(tn_ref.at[pl.ds(0, 5)], t_ref.at[pl.ds(0, 5)], st.at[0], rt.at[1], device(dz=5)).start()
+    copy(tn_ref, t_ref.at[pl.ds(10, 6)], st.at[0], rt.at[1], device(dz=-5)).start()
 
     arrived(b_ref, r1)
     for i in range(15):
@@ -230,6 +234,7 @@
     near = (1, -1, 2, -2)
     for i, d in enumerate(near):
         copy(z_ref.at[0], zn_ref.at[i], sz.at[0], rz.at[0], device(dz=d)).start()
+    pl.semaphore_wait(relay, 1)
     copy(z_ref.at[0], zn_ref.at[4], sz.at[0], rz.at[2], device(dz=8)).start()
 
     @pl.when(owner)
@@ -244,9 +249,26 @@
             copy(ez_ref.at[0], en_ref.at[i], es.at[1], er.at[1], device(dz=d)).start()
         copy(ez_ref.at[0], en_ref.at[4], es.at[1], er.at[3], device(dz=8)).start()
 
+    arrived(zn_ref.at[pl.ds(0, 4)], rz.at[0])
+    for i in range(4):
+        total = total + zn_ref[i]
+    z_ref[1] = total
+    for i, d in enumerate((5, -5)):
+        copy(z_ref.at[1], zf_ref.at[i], sz.at[1], rz.at[1], device(dz=d)).start()
+
+    @pl.when(owner)
+    def _():
+        arrived(en_ref.at[pl.ds(0, 4)], er.at[1])
+        acc = ez_ref[0]
+        for i in range(4):
+            acc = acc + en_ref[i]
+        ez_ref[1] = acc
+        for i, d in enumerate((5, -5)):
+            copy(ez_ref.at[1], ef_ref.at[i], es.at[2], er.at[2], device(dz=d)).start()
+
     arrived(t_ref.at[pl.ds(0, 11)], rt.at[1])
     for slot in range(16):
-        to_ref[(z + slot + 9) % 16] = t_ref[slot]
+        to_ref[(z + sign * (slot - 7) + 16) % 16] = tn_ref[slot - 5] if 5 <= slot < 10 else t_ref[slot]
     keep = pick(group, KEEP)
     kept = to_ref.at[pl.ds(keep * 8, 8)]
     given = to_ref.at[pl.ds((1 - keep) * 8, 8)]
@@ -254,23 +276,6 @@
     copy(given, tb_ref.at[core], st.at[2], rt.at[3], in_group(sent_to, core)).start()
     copy(given, tb_ref.at[core], st.at[2], rt.at[3], in_group(sent_to, other)).start()
     ta_ref[core] = to_ref[pl.ds(keep * 8, 8)]
-    arrived(zn_ref.at[pl.ds(0, 4)], rz.at[0])
-    for i in range(4):
-        total = total + zn_ref[i]
-    z_ref[1] = total
-    for i, d in enumerate((5, -5)):
-        copy(z_ref.at[1], zf_ref.at[i], sz.at[1], rz.at[1], device(dz=d)).start()
-
-    @pl.when(owner)
-    def _():
-        arrived(en_ref.at[pl.ds(0, 4)], er.at[1])
-        acc = ez_ref[0]
-        for i in range(4):
-            acc = acc + en_ref[i]
-        ez_ref[1] = acc
-        for i, d in enumerate((5, -5)):
-            copy(ez_ref.at[1], ef_ref.at[i], es.at[2], er.at[2], device(dz=d)).start()
-
     for layer in range(2):
         qt_ref[layer] = qk_ref[layer, 0].astype(F32).T.astype(BF16)
 
@@ -295,7 +300,7 @@
     total = total + zf_ref[0] + zf_ref[1] + zn_ref[4]
     piece_ref[...] = 2.0 * jax.nn.sigmoid(total) - targets
     for i, (dx, dy) in enumerate(OFFSETS):
-        copy(piece_ref, o_ref.at[core, mine], s3, r3.at[i], device(dx, dy)).start()
+        copy(piece_ref, o_ref.at[core, mine], s3, r3.at[GROUPS[i]], device(dx, dy)).start()
     copy(piece_ref, o_ref.at[core, mine], s4, r4, partner).start()
     o_ref[core, mine] = piece_ref[...]
 
@@ -310,11 +315,13 @@
         copy(ep_ref, eo_ref.at[core], es.at[4], er.at[5], partner).start()
         eo_ref[core] = ep_ref[...]
 
-    for i in reversed(range(15)):
-        dx, dy = OFFSETS[i]
-        piece = o_ref.at[core, place(-dx, -dy)]
-        arrived(piece, r3.at[i])
-        copy(piece, piece, s4, r4, partner).start()
+    for g in (3, 2, 1, 0):
+        members = [i for i in range(15) if GROUPS[i] == g]
+        arrived(y_ref.at[pl.ds(0, len(members))], r3.at[g])
+        for i in members:
+            dx, dy = OFFSETS[i]
+            piece = o_ref.at[core, place(-dx, -dy)]
+            copy(piece, piece, s4, r4, partner).start()
 
     @pl.when(jnp.logical_not(owner))
     def _():
@@ -326,10 +333,10 @@
     unpack(o_ref, eo_ref, s_ref)
 
     left(a_ref, s0)
-    left(y_ref, s1)
+    left(b_ref, s1)
     left(zn_ref, sz.at[0])
     left(zf_ref, sz.at[1])
-    left(t_ref.at[pl.ds(0, 15)], st.at[0])
+    left(t_ref, st.at[0])
     left(ta_ref.at[core], st.at[1])
     left(tb_ref, st.at[2])
     left(b_ref, s3)
@@ -368,6 +375,7 @@
     sums = lax.fori_loop(0, L // chunk, gather, (zero, zero), unroll=2)
     grads = []
     stores = []
+    h_rows = []
     for layer in range(2):
         h_row = jnp.sum(sums[layer], axis=0, keepdims=True)
         quad = jnp.sum(h_row * rr_ref[layer : layer + 1, :], axis=1, keepdims=True)
@@ -376,28 +384,56 @@
         for t in range(4):
             wide = jnp.broadcast_to(d_row[:, t * TILE : (t + 1) * TILE], (TILE, TILE))
             d_ref[layer, t * TILE : (t + 1) * TILE, :] = wide.T
-        acc = zero
-        for i in range(L // chunk):
-            rows = slice(i * chunk, (i + 1) * chunk)
-            s = s_ref[rows, :]
-            probs = p_ref[layer, rows, :]
-            wide = jnp.concatenate([d_ref[layer, rows, :]] * 4, axis=1)
-            dprobs = s + wide - h_scaled
-            prod = probs * s
-            for t in range(chunk // 8):
-                acc = acc + prod[t * 8 : (t + 1) * 8, :]
-            inner = jnp.sum(probs * dprobs, axis=1, keepdims=True)
-            ds_ref[layer, rows, :] = (probs * (dprobs - inner)).astype(BF16)
-        grads.append(jnp.sum(jnp.sum(acc, axis=0, keepdims=True), axis=1, keepdims=True) - quad * (0.5 / TOTAL))
-        factor = w_ref[layer : layer + 1, :] * scale
-        qg = jnp.dot(ds_ref[layer], qk_ref[layer, 1], preferred_element_type=F32)
-        qg_ref[layer] = (qg * factor).astype(BF16)
-        stores.append(pltpu.make_async_copy(qg_ref.at[layer], qg_hbm.at[layer], sems.at[2 * layer]))
+        h_rows.append(h_scaled)
+        grads.append(-quad * (0.5 / TOTAL))
+
+    def map_rows(layer, i, acc):
+        rows = slice(i * chunk, (i + 1) * chunk)
+        s = s_ref[rows, :]
+        probs = p_ref[layer, rows, :]
+        wide = jnp.concatenate([d_ref[layer, rows, :]] * 4, axis=1)
+        dprobs = s + wide - h_rows[layer]
+        prod = probs * s
+        for t in range(chunk // 8):
+            acc = acc + prod[t * 8 : (t + 1) * 8, :]
+        inner = jnp.sum(probs * dprobs, axis=1, keepdims=True)
+        ds_ref[layer, rows, :] = (probs * (dprobs - inner)).astype(BF16)
+        return acc
+
+    def query_rows(layer, i, count):
+        rows = slice(i * count, (i + 1) * count)
+        qg = jnp.dot(ds_ref[layer, rows, :], qk_ref[layer, 1], preferred_element_type=F32)
+        qg_ref[layer, rows, :] = (qg * (w_ref[layer : layer + 1, :] * scale)).astype(BF16)
+
+    def key_rows(layer, i, count):
+        rows = slice(i * count, (i + 1) * count)
+        kg = jnp.dot(qt_ref[layer], ds_ref[layer, :, rows], preferred_element_type=F32)
+        kg_ref[layer, rows, :] = (kg.T * (w_ref[layer : layer + 1, :] * scale)).astype(BF16)
+
+    def store(src, dst, index):
+        stores.append(pltpu.make_async_copy(src, dst, sems.at[index]))
         stores[-1].start()
-        kg = jnp.dot(qt_ref[layer], ds_ref[layer], preferred_element_type=F32)
-        kg_ref[layer] = (kg.T * factor).astype(BF16)
-        stores.append(pltpu.make_async_copy(kg_ref.at[layer], kg_hbm.at[layer], sems.at[2 * layer + 1]))
-        stores[-1].start()
+
+    acc = zero
+    for i in range(16):
+        acc = map_rows(0, i, acc)
+    grads[0] = grads[0] + jnp.sum(jnp.sum(acc, axis=0, keepdims=True), axis=1, keepdims=True)
+    acc = zero
+    for i in range(16):
+        acc = map_rows(1, i, acc)
+        if i % 8 == 3:
+            query_rows(0, i // 8, 256)
+        if i % 8 == 7:
+            key_rows(0, i // 8, 256)
+    grads[1] = grads[1] + jnp.sum(jnp.sum(acc, axis=0, keepdims=True), axis=1, keepdims=True)
+    store(qg_ref.at[0], qg_hbm.at[0], 0)
+    store(kg_ref.at[0], kg_hbm.at[0], 1)
+    for i in range(2):
+        key_rows(1, i, 256)
+    store(kg_ref.at[1], kg_hbm.at[1], 2)
+    for i in range(2):
+        query_rows(1, i, 256)
+    store(qg_ref.at[1], qg_hbm.at[1], 3)
     lane = lax.broadcasted_iota(jnp.int32, (1, 2), 1)
     wg_ref[...] = jnp.where(lane == 0, grads[0], grads[1])
     for c in stores:
@@ -441,9 +477,10 @@
             pltpu.VMEM((16 * ROWS + 8, TILE), F32),
             pltpu.VMEM((15, ROWS, TILE), F32),
             pltpu.VMEM((15, ROWS, TILE), F32),
-            pltpu.VMEM((2, ROWS, TILE), F32),
+            pltpu.VMEM((3, ROWS, TILE), F32),
             pltpu.VMEM((5, ROWS, TILE), F32),
             pltpu.VMEM((2, ROWS, TILE), F32),
+            pltpu.VMEM((6, 8, TILE), jnp.int32),
             pltpu.VMEM((16, 8, TILE), jnp.int32),
             pltpu.VMEM((16, 8, TILE), jnp.int32),
             pltpu.VMEM((2, 8, 8, TILE), jnp.int32),
@@ -454,13 +491,13 @@
             pltpu.VMEM((2, 8, TILE), F32),
             pltpu.VMEM((8, TILE), F32),
             pltpu.VMEM((16, 8, TILE), F32),
-            pltpu.VMEM((2, 8, TILE), F32),
+            pltpu.VMEM((3, 8, TILE), F32),
             pltpu.VMEM((5, 8, TILE), F32),
             pltpu.VMEM((2, 8, TILE), F32),
             pltpu.VMEM((8, TILE), F32),
             pltpu.VMEM((2, 8, TILE), F32),
-            dma((4,)), dma, dma((4,)), dma, dma, dma((2,)), dma((3,)), dma((3,)), dma((4,)),
-            dma, dma((15,)), dma, dma, dma((5,)), dma((6,)),
+            dma((4,)), dma, dma((5,)), dma, dma, dma((2,)), dma((3,)), dma((3,)), dma((4,)),
+            dma, dma((4,)), dma, dma, dma((5,)), dma((6,)), pltpu.SemaphoreType.REGULAR,
         ],
         compiler_params=pltpu.CompilerParams(collective_id=0, has_side_effects=True, vmem_limit_bytes=16 << 20),
     )(slot_head, *[pltpu.with_memory_space_constraint(v, pltpu.HBM) for v in (head_weight, target, q, k)])

time: 45.3 us -> 43.8 us (0.967)
  Pallas kernels: 43.9 us -> 42.4 us
    pallas_call x1, Pallas kernels: 41.2 us -> 39.6 us  [on_device(): pl.pallas_call(exchange_kernel, out_shape=(pltpu.VMEM((2, L, L), F32), pl...]
where the time goes in v3:
time: 43.8 us; the launch traced here: 43.7 us
  Pallas kernels  42.4 us (97%)
  between operations  1.29 us (3%)
    pallas_call x1, Pallas kernels, on_device(): pl.pallas_call(exchange_kernel, out_shape=(pltpu.VMEM((2, L, L), F32), pl...  39.6 us
    pallas_call x1, Pallas kernels, on_device(): pl.pallas_call(back_kernel, out_shape=(jax.ShapeDtypeStruct((2, L, DH), B...  2.79 us

profile of v3, /device:TPU:1, one launch (start us, length us, event | category | flops | bytes accessed | tf_op | source)
XLA Modules:
  0.0 43.7 jit_solution(14014381027678837096)
XLA Ops:
  1.3 39.6 %shard_map.76 = (f32[2,512,512]{2,1,0:T(8,128)S(1)}, f32[512,512]{1,0:T(8,128)S(1)}, f32[2,512,128]{2,1,0:T(8,128)S(1)}, f32[2,512]{1,0:T(2,128)S(1)}, f32[2,128...) custom-call(s32[1]{0:T(128)S(6)} %copy.10.slot_ref, f32[2,40]{1,0:T(2,128)} %hw_hbm.1, ...), custom_call_target="tpu_custom_call" | custom-call | tf_op jit(solution)/shard_map/pallas_call | solution.py:459
  40.9 2.8 %shard_map.77 = (bf16[2,512,128]{2,1,0:T(8,128)(2,1)}, bf16[2,512,128]{2,1,0:T(8,128)(2,1)}, f32[1,2]{1,0:T(1,128)}) custom-call(f32[2,128]{1,0:T(2,128)S(1)} %get-tuple-element.13.w_ref, bf16[2,128,512]{2,1,0:T(8,128)(2,1)S(1)} %get-tuple-element.14.qt_ref, bf16[2,2,512,128]{3,2,1,0:T(8,128)(2,1)S(1)} %get-tuple-element.15.qk_ref, ...), custom_call_target="tpu_custom_call" | custom-call | tf_op jit(solution)/shard_map/pallas_call | solution.py:504

commit v4 on v3

--- a/solution.py
+++ b/solution.py
@@ -23,8 +23,6 @@
     key=lambda o: -(min(o[0], 4 - o[0]) + min(o[1], 4 - o[1])),
 )
 
-GROUPS = (0,) * 5 + (1,) * 3 + (2,) * 3 + (3,) * 4
-
 
 def pick(index, table):
     value = jnp.int32(table[0])
@@ -45,13 +43,14 @@
     sums = []
     for layer in range(2):
         ready(layer)
-        sc_ref[...] = lax.dot_general(
+        sc_ref[layer] = lax.dot_general(
             qk_ref[layer, 0], qk_ref[layer, 1], (((1,), (1,)), ((), ())), preferred_element_type=F32
         )
+    for layer in range(2):
 
         def body(i, csum, layer=layer):
             rows = pl.ds(pl.multiple_of(i * chunk, chunk), chunk)
-            scores = sc_ref[rows, :]
+            scores = sc_ref[layer, rows, :]
             highest = jnp.max(scores, axis=1, keepdims=True)
             expo = jnp.exp((scores - highest) * scale)
             probs = expo * (1.0 / jnp.sum(expo, axis=1, keepdims=True))
@@ -146,19 +145,23 @@
     sign = 1 - 2 * core
 
     def device(dx=0, dy=0, dz=0, flip=False):
-        nx = (x + dx) % 4
-        ny = (y + dy) % 4
+        nx = (x + sign * dx + 4) % 4
+        ny = (y + sign * dy + 4) % 4
         nz = (z + sign * dz + 16) % 16
         nc = other if flip else core
         return {"layer": (ny % 2) * 4 + nx, "head": (ny // 2) * 32 + nz * 2 + nc}
 
     def place(dx, dy):
-        nx = (x + dx) % 4
-        ny = (y + dy) % 4
+        nx = (x + sign * dx + 4) % 4
+        ny = (y + sign * dy + 4) % 4
         return ((ny // 2) * 4 + nx) * 2 + ny % 2
 
     def in_group(g, c):
-        return {"layer": y_lo * 4 + g % 4, "head": (g // 4) * 32 + z * 2 + c}
+        low = (y_lo + g // 4 + y_hi) % 2
+        return {"layer": low * 4 + g % 4, "head": (g // 4) * 32 + z * 2 + c}
+
+    def chip(p):
+        return {"layer": (p % 2) * 4 + (p // 2) % 4, "head": (p // 8) * 32 + z * 2 + core}
 
     partner = device(flip=True)
     sent_to = pick(group, MIRROR)
@@ -201,7 +204,7 @@
     order = OFFSETS + [(0, 0)]
     copy(e_ref.at[other], a_ref.at[pl.ds(16 * ROWS, 8)], s0, r0.at[0], partner).start()
     for i, (dx, dy) in enumerate(order):
-        copy(x_ref.at[other, place(dx, dy)], a_ref.at[pl.ds(i * ROWS, ROWS)], s0, r0.at[1 + i // 4], partner).start()
+        copy(x_ref.at[other, place(-dx, -dy)], a_ref.at[pl.ds(i * ROWS, ROWS)], s0, r0.at[1 + i // 4], partner).start()
 
     arrived(a_ref.at[pl.ds(16 * ROWS, 8)], r0.at[0])
     ey_ref[...] = e_ref[core] + a_ref[16 * ROWS : 16 * ROWS + 8, :]
@@ -299,10 +302,14 @@
     arrived(zn_ref.at[4], rz.at[2])
     total = total + zf_ref[0] + zf_ref[1] + zn_ref[4]
     piece_ref[...] = 2.0 * jax.nn.sigmoid(total) - targets
-    for i, (dx, dy) in enumerate(OFFSETS):
-        copy(piece_ref, o_ref.at[core, mine], s3, r3.at[GROUPS[i]], device(dx, dy)).start()
-    copy(piece_ref, o_ref.at[core, mine], s4, r4, partner).start()
-    o_ref[core, mine] = piece_ref[...]
+    for p in range(16):
+
+        @pl.when(mine != p)
+        def _(p=p):
+            copy(piece_ref, o_ref.at[core, mine], s3, r3.at[mine // 4], chip(p)).start()
+
+    keep_own = pltpu.make_async_copy(piece_ref, o_ref.at[core, mine], r3.at[mine // 4])
+    keep_own.start()
 
     @pl.when(owner)
     def _():
@@ -315,13 +322,10 @@
         copy(ep_ref, eo_ref.at[core], es.at[4], er.at[5], partner).start()
         eo_ref[core] = ep_ref[...]
 
-    for g in (3, 2, 1, 0):
-        members = [i for i in range(15) if GROUPS[i] == g]
-        arrived(y_ref.at[pl.ds(0, len(members))], r3.at[g])
-        for i in members:
-            dx, dy = OFFSETS[i]
-            piece = o_ref.at[core, place(-dx, -dy)]
-            copy(piece, piece, s4, r4, partner).start()
+    for g in range(4):
+        pieces = o_ref.at[core, pl.ds(4 * g, 4)]
+        arrived(pieces, r3.at[g])
+        copy(pieces, pieces, s4, r4, partner).start()
 
     @pl.when(jnp.logical_not(owner))
     def _():
@@ -354,7 +358,7 @@
         left(ey_ref, es.at[0])
 
 
-def back_kernel(w_ref, qt_ref, qk_ref, p_ref, s_ref, rb_ref, rr_ref, qg_hbm, kg_hbm, wg_ref, d_ref, ds_ref, qg_ref, kg_ref, sems):
+def back_kernel(w_ref, qt_ref, qk_ref, p_ref, s_ref, rb_ref, rr_ref, qg_hbm, kg_hbm, wg_hbm, d_ref, ds_ref, qg_ref, kg_ref, wg_ref, sems):
     scale = DH ** (-0.5)
     chunk = 32
     zero = jnp.zeros((8, L), F32)
@@ -426,6 +430,9 @@
         if i % 8 == 7:
             key_rows(0, i // 8, 256)
     grads[1] = grads[1] + jnp.sum(jnp.sum(acc, axis=0, keepdims=True), axis=1, keepdims=True)
+    lane = lax.broadcasted_iota(jnp.int32, (1, 2), 1)
+    wg_ref[...] = jnp.where(lane == 0, grads[0], grads[1])
+    store(wg_ref, wg_hbm, 5)
     store(qg_ref.at[0], qg_hbm.at[0], 0)
     store(kg_ref.at[0], kg_hbm.at[0], 1)
     for i in range(2):
@@ -433,9 +440,8 @@
     store(kg_ref.at[1], kg_hbm.at[1], 2)
     for i in range(2):
         query_rows(1, i, 256)
-    store(qg_ref.at[1], qg_hbm.at[1], 3)
-    lane = lax.broadcasted_iota(jnp.int32, (1, 2), 1)
-    wg_ref[...] = jnp.where(lane == 0, grads[0], grads[1])
+        rows = pl.ds(i * 256, 256)
+        store(qg_ref.at[1, rows], qg_hbm.at[1, rows], 3 + i)
     for c in stores:
         c.wait()
 
@@ -472,7 +478,7 @@
         scratch_shapes=[
             pltpu.VMEM((2, 40), F32),
             pltpu.VMEM((8, L), jnp.int32),
-            pltpu.VMEM((L, L), F32),
+            pltpu.VMEM((2, L, L), F32),
             pltpu.VMEM((2, 16, ROWS, TILE), F32),
             pltpu.VMEM((16 * ROWS + 8, TILE), F32),
             pltpu.VMEM((15, ROWS, TILE), F32),
@@ -509,13 +515,14 @@
             jax.ShapeDtypeStruct((1, 2), F32),
         ),
         in_specs=[vmem()] * 7,
-        out_specs=(hbm(), hbm(), vmem()),
+        out_specs=(hbm(), hbm(), hbm()),
         scratch_shapes=[
             pltpu.VMEM((2, L, TILE), F32),
             pltpu.VMEM((2, L, L), BF16),
             pltpu.VMEM((2, L, DH), BF16),
             pltpu.VMEM((2, L, DH), BF16),
-            pltpu.SemaphoreType.DMA((4,)),
+            pltpu.VMEM((1, 2), F32),
+            pltpu.SemaphoreType.DMA((6,)),
         ],
         compiler_params=pltpu.CompilerParams(vmem_limit_bytes=16 << 20),
     )(w, q_turned, qk, probs, s_map, rb, rr)

time: 43.8 us -> 43.4 us (level)
  Pallas kernels: 42.4 us -> 41.9 us
    pallas_call x1, Pallas kernels: 2.79 us -> 2.3 us  [on_device(): pl.pallas_call(back_kernel, out_shape=(jax.ShapeDtypeStruct((2, L, DH), B...]
where the time goes in v4:
time: 43.4 us; the launch traced here: 43.2 us
  Pallas kernels  41.9 us (97%)
  between operations  1.29 us (3%)
    pallas_call x1, Pallas kernels, on_device(): pl.pallas_call(exchange_kernel, out_shape=(pltpu.VMEM((2, L, L), F32), pl...  39.6 us
    pallas_call x1, Pallas kernels, on_device(): pl.pallas_call(back_kernel, out_shape=(jax.ShapeDtypeStruct((2, L, DH), B...  2.3 us

profile of v4, /device:TPU:1, one launch (start us, length us, event | category | flops | bytes accessed | tf_op | source)
XLA Modules:
  0.0 43.2 jit_solution(8805386782708586)
XLA Ops:
  1.3 39.6 %shard_map.76 = (f32[2,512,512]{2,1,0:T(8,128)S(1)}, f32[512,512]{1,0:T(8,128)S(1)}, f32[2,512,128]{2,1,0:T(8,128)S(1)}, f32[2,512]{1,0:T(2,128)S(1)}, f32[2,128...) custom-call(s32[1]{0:T(128)S(6)} %copy.10.slot_ref, f32[2,40]{1,0:T(2,128)} %hw_hbm.1, ...), custom_call_target="tpu_custom_call" | custom-call | tf_op jit(solution)/shard_map/pallas_call | solution.py:465
  40.9 2.3 %shard_map.77 = (bf16[2,512,128]{2,1,0:T(8,128)(2,1)}, bf16[2,512,128]{2,1,0:T(8,128)(2,1)}, f32[1,2]{1,0:T(1,128)}) custom-call(f32[2,128]{1,0:T(2,128)S(1)} %get-tuple-element.13.w_ref, bf16[2,128,512]{2,1,0:T(8,128)(2,1)S(1)} %get-tuple-element.14.qt_ref, bf16[2,2,512,128]{3,2,1,0:T(8,128)(2,1)S(1)} %get-tuple-element.15.qk_ref, ...), custom_call_target="tpu_custom_call" | custom-call | tf_op jit(solution)/shard_map/pallas_call | solution.py:510

commit v5 on v4

--- a/solution.py
+++ b/solution.py
@@ -91,31 +91,43 @@
             x_ref[part % 2, 2 * g + part // 2] = full[part * ROWS : (part + 1) * ROWS, :]
 
 
-def unpack(o_ref, eo_ref, s_ref):
+def unpack(o_ref, eo_ref, rb_ref, s_ref, h_ref):
     row = lax.broadcasted_iota(jnp.int32, (TILE, TILE), 0)
     col = lax.broadcasted_iota(jnp.int32, (TILE, TILE), 1)
 
     def cut(t):
         return slice(t * TILE, (t + 1) * TILE)
+
+    sums = [[jnp.zeros((8, TILE), F32)] * 4 for _ in range(2)]
+
+    def put(a, b, value):
+        s_ref[cut(a), cut(b)] = value
+        for layer in range(2):
+            weighted = rb_ref[layer, cut(a), :] * value
+            for t in range(TILE // 8):
+                sums[layer][b] = sums[layer][b] + weighted[t * 8 : (t + 1) * 8, :]
 
     for g in range(8):
         full = jnp.concatenate([o_ref[part % 2, 2 * g + part // 2] for part in range(4)], axis=0)
         if g in OFF:
             a, b = OFF[g]
-            s_ref[cut(a), cut(b)] = full
-            s_ref[cut(b), cut(a)] = full.T
+            put(a, b, full)
+            put(b, a, full.T)
         else:
             a, b = DIAG[g]
             turned = full.T
             diagonal = eo_ref[g // 7, 0:1, :]
             upper = jnp.where(row < col, full, jnp.where(row == col, diagonal, turned))
-            s_ref[cut(a), cut(a)] = upper
-            s_ref[cut(b), cut(b)] = jnp.where(row < col, turned, full)
+            put(a, a, upper)
+            put(b, b, jnp.where(row < col, turned, full))
+    for layer in range(2):
+        for t in range(4):
+            h_ref[layer, :, cut(t)] = sums[layer][t]
 
 
 def exchange_kernel(
     slot_ref, hw_hbm, target_hbm, q_hbm, k_hbm,
-    p_ref, s_ref, rb_ref, rr_ref, w_ref, qk_ref, qt_ref,
+    p_ref, s_ref, h_ref, rr_ref, w_ref, qk_ref, qt_ref, rb_ref,
     hw_ref, target_ref, sc_ref, x_ref, a_ref, y_ref, b_ref, z_ref, zn_ref, zf_ref,
     tn_ref, t_ref, to_ref, ta_ref, tb_ref, tt_ref, piece_ref, o_ref,
     e_ref, ey_ref, eb_ref, ez_ref, en_ref, ef_ref, ep_ref, eo_ref,
@@ -197,8 +209,9 @@
         copy(ref, ref, ssem, r1, partner).wait_send()
 
     tile = target_ref.at[:, pl.ds(pl.multiple_of(x * TILE, TILE), TILE)]
-    for d, slot in ((1, 1), (-1, 3), (2, 0), (-2, 4), (-3, 5)):
+    for d, slot in ((1, 1), (-1, 3), (2, 0), (-2, 4)):
         copy(tile, tn_ref.at[slot], st.at[0], rt.at[0], device(dz=d)).start()
+    copy(tile, tn_ref.at[5], st.at[0], rt.at[4], device(dz=-3)).start()
     tn_ref[2] = target_ref[:, pl.ds(pl.multiple_of(x * TILE, TILE), TILE)]
 
     order = OFFSETS + [(0, 0)]
@@ -225,9 +238,10 @@
         else:
             total = summed
 
-    arrived(t_ref.at[pl.ds(0, 5)], rt.at[0])
+    arrived(t_ref.at[pl.ds(0, 4)], rt.at[0])
     pl.semaphore_signal(relay, inc=1, device_id=device(dz=-5), device_id_type=MESH)
     copy(tn_ref.at[pl.ds(0, 5)], t_ref.at[pl.ds(0, 5)], st.at[0], rt.at[1], device(dz=5)).start()
+    arrived(tn_ref.at[5], rt.at[4])
     copy(tn_ref, t_ref.at[pl.ds(10, 6)], st.at[0], rt.at[1], device(dz=-5)).start()
 
     arrived(b_ref, r1)
@@ -237,9 +251,6 @@
     near = (1, -1, 2, -2)
     for i, d in enumerate(near):
         copy(z_ref.at[0], zn_ref.at[i], sz.at[0], rz.at[0], device(dz=d)).start()
-    pl.semaphore_wait(relay, 1)
-    copy(z_ref.at[0], zn_ref.at[4], sz.at[0], rz.at[2], device(dz=8)).start()
-
     @pl.when(owner)
     def _():
         eb_ref[mine] = ey_ref[...]
@@ -250,6 +261,12 @@
         ez_ref[0] = acc
         for i, d in enumerate(near):
             copy(ez_ref.at[0], en_ref.at[i], es.at[1], er.at[1], device(dz=d)).start()
+
+    pl.semaphore_wait(relay, 1)
+    copy(z_ref.at[0], zn_ref.at[4], sz.at[0], rz.at[2], device(dz=8)).start()
+
+    @pl.when(owner)
+    def _():
         copy(ez_ref.at[0], en_ref.at[4], es.at[1], er.at[3], device(dz=8)).start()
 
     arrived(zn_ref.at[pl.ds(0, 4)], rz.at[0])
@@ -334,7 +351,7 @@
 
     arrived(o_ref.at[other], r4)
     arrived(eo_ref.at[other], er.at[5])
-    unpack(o_ref, eo_ref, s_ref)
+    unpack(o_ref, eo_ref, rb_ref, s_ref, h_ref)
 
     left(a_ref, s0)
     left(b_ref, s1)
@@ -358,30 +375,16 @@
         left(ey_ref, es.at[0])
 
 
-def back_kernel(w_ref, qt_ref, qk_ref, p_ref, s_ref, rb_ref, rr_ref, qg_hbm, kg_hbm, wg_hbm, d_ref, ds_ref, qg_ref, kg_ref, wg_ref, sems):
+def back_kernel(w_ref, qt_ref, qk_ref, p_ref, s_ref, h_ref, rr_ref, qg_hbm, kg_hbm, wg_hbm, d_ref, ds_ref, qg_ref, kg_ref, wg_ref, sems):
     scale = DH ** (-0.5)
     chunk = 32
     zero = jnp.zeros((8, L), F32)
 
-    def gather(i, carry):
-        rows = pl.ds(pl.multiple_of(i * chunk, chunk), chunk)
-        s = s_ref[rows, :]
-        out = []
-        for layer in range(2):
-            wide = jnp.concatenate([rb_ref[layer, rows, :]] * 4, axis=1)
-            prod = s * wide
-            acc = carry[layer]
-            for t in range(chunk // 8):
-                acc = acc + prod[t * 8 : (t + 1) * 8, :]
-            out.append(acc)
-        return tuple(out)
-
-    sums = lax.fori_loop(0, L // chunk, gather, (zero, zero), unroll=2)
     grads = []
     stores = []
     h_rows = []
     for layer in range(2):
-        h_row = jnp.sum(sums[layer], axis=0, keepdims=True)
+        h_row = jnp.sum(h_ref[layer], axis=0, keepdims=True)
         quad = jnp.sum(h_row * rr_ref[layer : layer + 1, :], axis=1, keepdims=True)
         h_scaled = h_row * (1.0 / TOTAL)
         d_row = quad * (1.0 / (TOTAL * TOTAL)) - h_scaled
@@ -462,12 +465,12 @@
     q = queries.reshape(2, L, DH)
     k = keys.reshape(2, L, DH)
     dma = pltpu.SemaphoreType.DMA
-    probs, s_map, rb, rr, w, qk, q_turned = pl.pallas_call(
+    probs, s_map, h, rr, w, qk, q_turned = pl.pallas_call(
         exchange_kernel,
         out_shape=(
             pltpu.VMEM((2, L, L), F32),
             pltpu.VMEM((L, L), F32),
-            pltpu.VMEM((2, L, TILE), F32),
+            pltpu.VMEM((2, 8, L), F32),
             pltpu.VMEM((2, L), F32),
             pltpu.VMEM((2, TILE), F32),
             pltpu.VMEM((2, 2, L, DH), BF16),
@@ -476,6 +479,7 @@
         in_specs=[smem()] + [hbm()] * 4,
         out_specs=(vmem(),) * 7,
         scratch_shapes=[
+            pltpu.VMEM((2, L, TILE), F32),
             pltpu.VMEM((2, 40), F32),
             pltpu.VMEM((8, L), jnp.int32),
             pltpu.VMEM((2, L, L), F32),
@@ -502,7 +506,7 @@
             pltpu.VMEM((2, 8, TILE), F32),
             pltpu.VMEM((8, TILE), F32),
             pltpu.VMEM((2, 8, TILE), F32),
-            dma((4,)), dma, dma((5,)), dma, dma, dma((2,)), dma((3,)), dma((3,)), dma((4,)),
+            dma((4,)), dma, dma((5,)), dma, dma, dma((2,)), dma((3,)), dma((3,)), dma((5,)),
             dma, dma((4,)), dma, dma, dma((5,)), dma((6,)), pltpu.SemaphoreType.REGULAR,
         ],
         compiler_params=pltpu.CompilerParams(collective_id=0, has_side_effects=True, vmem_limit_bytes=16 << 20),
@@ -525,7 +529,7 @@
             pltpu.SemaphoreType.DMA((6,)),
         ],
         compiler_params=pltpu.CompilerParams(vmem_limit_bytes=16 << 20),
-    )(w, q_turned, qk, probs, s_map, rb, rr)
+    )(w, q_turned, qk, probs, s_map, h, rr)
     return (qg.reshape(2, 1, L, DH), kg.reshape(2, 1, L, DH), wg.reshape(2, 1))
 
 

time: 43.4 us -> 42.8 us (0.986)
  Pallas kernels: 41.9 us -> 41.3 us
where the time goes in v5:
time: 42.8 us; the launch traced here: 42.6 us
  Pallas kernels  41.3 us (96%)
  between operations  1.29 us (3%)
    pallas_call x1, Pallas kernels, on_device(): pl.pallas_call(exchange_kernel, out_shape=(pltpu.VMEM((2, L, L), F32), pl...  39.2 us
    pallas_call x1, Pallas kernels, on_device(): pl.pallas_call(back_kernel, out_shape=(jax.ShapeDtypeStruct((2, L, DH), B...  2.14 us

profile of v5, /device:TPU:1, one launch (start us, length us, event | category | flops | bytes accessed | tf_op | source)
XLA Modules:
  0.0 42.6 jit_solution(1870335239068565943)
XLA Ops:
  1.3 39.2 %shard_map.76 = (f32[2,512,512]{2,1,0:T(8,128)S(1)}, f32[512,512]{1,0:T(8,128)S(1)}, f32[2,8,512]{2,1,0:T(8,128)S(1)}, f32[2,512]{1,0:T(2,128)S(1)}, f32[2,128]{...) custom-call(s32[1]{0:T(128)S(6)} %copy.10.slot_ref, f32[2,40]{1,0:T(2,128)} %hw_hbm.1, ...), custom_call_target="tpu_custom_call" | custom-call | tf_op jit(solution)/shard_map/pallas_call | solution.py:468
  40.5 2.1 %shard_map.77 = (bf16[2,512,128]{2,1,0:T(8,128)(2,1)}, bf16[2,512,128]{2,1,0:T(8,128)(2,1)}, f32[1,2]{1,0:T(1,128)}) custom-call(f32[2,128]{1,0:T(2,128)S(1)} %get-tuple-element.13.w_ref, bf16[2,128,512]{2,1,0:T(8,128)(2,1)S(1)} %get-tuple-element.14.qt_ref, bf16[2,2,512,128]{3,2,1,0:T(8,128)(2,1)S(1)} %get-tuple-element.15.qk_ref, ...), custom_call_target="tpu_custom_call" | custom-call | tf_op jit(solution)/shard_map/pallas_call | solution.py:514

commit v6 on v5

--- a/solution.py
+++ b/solution.py
@@ -424,14 +424,19 @@
     acc = zero
     for i in range(16):
         acc = map_rows(0, i, acc)
+        if i == 9:
+            query_rows(0, 0, 256)
     grads[0] = grads[0] + jnp.sum(jnp.sum(acc, axis=0, keepdims=True), axis=1, keepdims=True)
     acc = zero
     for i in range(16):
         acc = map_rows(1, i, acc)
-        if i % 8 == 3:
-            query_rows(0, i // 8, 256)
-        if i % 8 == 7:
-            key_rows(0, i // 8, 256)
+        if i == 1:
+            query_rows(0, 1, 256)
+        if i == 3 or i == 7:
+            key_rows(0, i // 4, 256)
+        if i == 9:
+            query_rows(1, 0, 256)
+            store(qg_ref.at[1, pl.ds(0, 256)], qg_hbm.at[1, pl.ds(0, 256)], 3)
     grads[1] = grads[1] + jnp.sum(jnp.sum(acc, axis=0, keepdims=True), axis=1, keepdims=True)
     lane = lax.broadcasted_iota(jnp.int32, (1, 2), 1)
     wg_ref[...] = jnp.where(lane == 0, grads[0], grads[1])
@@ -441,10 +446,8 @@
     for i in range(2):
         key_rows(1, i, 256)
     store(kg_ref.at[1], kg_hbm.at[1], 2)
-    for i in range(2):
-        query_rows(1, i, 256)
-        rows = pl.ds(i * 256, 256)
-        store(qg_ref.at[1, rows], qg_hbm.at[1, rows], 3 + i)
+    query_rows(1, 1, 256)
+    store(qg_ref.at[1, pl.ds(256, 256)], qg_hbm.at[1, pl.ds(256, 256)], 4)
     for c in stores:
         c.wait()
 

time: 42.8 us -> 42.7 us (level)
  no operation moved by 1% of the time
where the time goes in v6:
time: 42.7 us; the launch traced here: 42.6 us
  Pallas kernels  41.3 us (97%)
  between operations  1.29 us (3%)
    pallas_call x1, Pallas kernels, on_device(): pl.pallas_call(exchange_kernel, out_shape=(pltpu.VMEM((2, L, L), F32), pl...  39.2 us
    pallas_call x1, Pallas kernels, on_device(): pl.pallas_call(back_kernel, out_shape=(jax.ShapeDtypeStruct((2, L, DH), B...  2.08 us

profile of v6, /device:TPU:1, one launch (start us, length us, event | category | flops | bytes accessed | tf_op | source)
XLA Modules:
  0.0 42.6 jit_solution(5806169403976832490)
XLA Ops:
  1.3 39.2 %shard_map.76 = (f32[2,512,512]{2,1,0:T(8,128)S(1)}, f32[512,512]{1,0:T(8,128)S(1)}, f32[2,8,512]{2,1,0:T(8,128)S(1)}, f32[2,512]{1,0:T(2,128)S(1)}, f32[2,128]{...) custom-call(s32[1]{0:T(128)S(6)} %copy.10.slot_ref, f32[2,40]{1,0:T(2,128)} %hw_hbm.1, ...), custom_call_target="tpu_custom_call" | custom-call | tf_op jit(solution)/shard_map/pallas_call | solution.py:471
  40.5 2.1 %shard_map.77 = (bf16[2,512,128]{2,1,0:T(8,128)(2,1)}, bf16[2,512,128]{2,1,0:T(8,128)(2,1)}, f32[1,2]{1,0:T(1,128)}) custom-call(f32[2,128]{1,0:T(2,128)S(1)} %get-tuple-element.13.w_ref, bf16[2,128,512]{2,1,0:T(8,128)(2,1)S(1)} %get-tuple-element.14.qt_ref, bf16[2,2,512,128]{3,2,1,0:T(8,128)(2,1)S(1)} %get-tuple-element.15.qk_ref, ...), custom_call_target="tpu_custom_call" | custom-call | tf_op jit(solution)/shard_map/pallas_call | solution.py:517
